TPU v7x, 32 devices: a whole 2x2x4 slice. The times are simulated.
32 devices in a mesh: ctx: 8 (over y, x, core), fsdp: 4 (over z).
Axes of the slice: x: 2, y: 2, z: 4, core: 2. Of those that a mesh axis runs over, the one named last changes fastest.
Arguments:
- hidden: bfloat16 [4096, 1536], P(('fsdp', 'ctx')), may hold values from -6 to 6
- positions: int32 [4096], P('fsdp'), may hold values from 0 to 1023, as said below
- first_gain: bfloat16 [1536], P(('ctx', 'fsdp')), may hold values from 0.099609375 to 1.8984375
- query_weight: bfloat16 [1536, 1536], P(('ctx', 'fsdp')), may hold values from -0.15625 to 0.15625
- key_weight: bfloat16 [1536, 256], P(('ctx', 'fsdp')), may hold values from -0.15625 to 0.15625
- value_weight: bfloat16 [1536, 256], P(('ctx', 'fsdp')), may hold values from -0.15625 to 0.15625
- query_bias: bfloat16 [1536], P(('ctx', 'fsdp')), may hold values from -3 to 3
- key_bias: bfloat16 [256], P(('ctx', 'fsdp')), may hold values from -3 to 3
- value_bias: bfloat16 [256], P(('ctx', 'fsdp')), may hold values from -3 to 3
- output_weight: bfloat16 [1536, 1536], P(('ctx', 'fsdp')), may hold values from -0.625 to 0.625
- second_gain: bfloat16 [1536], P(('ctx', 'fsdp')), may hold values from 0.099609375 to 1.8984375
- gate_weight: bfloat16 [1536, 8960], P(None, ('ctx', 'fsdp')), may hold values from -0.15625 to 0.15625
- up_weight: bfloat16 [1536, 8960], P(None, ('ctx', 'fsdp')), may hold values from -0.15625 to 0.15625
- down_weight: bfloat16 [8960, 1536], P(('ctx', 'fsdp')), may hold values from -0.0625 to 0.0625
- cotangent: bfloat16 [4096, 1536], P(('fsdp', 'ctx')), may hold values from -6 to 6
Outputs:
- layer_output: bfloat16 [4096, 1536], P(('fsdp', 'ctx'))
- input_gradient: float32 [4096, 1536], P(('fsdp', 'ctx'))
- first_gain_gradient: float32 [1536], P(('ctx', 'fsdp'))
- query_weight_gradient: float32 [1536, 1536], P(('ctx', 'fsdp'))
- key_weight_gradient: float32 [1536, 256], P(('ctx', 'fsdp'))
- value_weight_gradient: float32 [1536, 256], P(('ctx', 'fsdp'))
- query_bias_gradient: float32 [1536], P(('ctx', 'fsdp'))
- key_bias_gradient: float32 [256], P(('ctx', 'fsdp'))
- value_bias_gradient: float32 [256], P(('ctx', 'fsdp'))
- output_weight_gradient: float32 [1536, 1536], P(('ctx', 'fsdp'))
- second_gain_gradient: float32 [1536], P(('ctx', 'fsdp'))
- gate_weight_gradient: float32 [1536, 8960], P(None, ('ctx', 'fsdp'))
- up_weight_gradient: float32 [1536, 8960], P(None, ('ctx', 'fsdp'))
- down_weight_gradient: float32 [8960, 1536], P(('ctx', 'fsdp'))
Inputs may be any that keep to these rules, and one draw needn't show every extreme that they name: Within each sequence of 1024 tokens, the 128 tokens of each index of ctx are two runs of consecutive positions of 64 each: blocks b and 15 - b of the sequence cut into 16 equal blocks, the earlier block first, where b (0 to 7) may differ for each index of ctx and each sequence; every position of the sequence appears once.
All inputs are finite; a program needn't handle non-finite values.
Results may differ from a plain program's by a relative error of at most 0.035.
Values may be sent and summed in bfloat16 or wider, within the bound.
No kernel may reach another device: no remote copies, remote signals or barrier semaphores. Data moves between devices by JAX's collectives and lax.ppermute only.
A program may use at most 256 MiB of HBM per device.

v0:
```python
import jax
import jax.numpy as jnp
from jax import lax
from jax.experimental import pallas as pl
from jax.experimental.pallas import tpu as pltpu
from jax.sharding import Mesh
from jax.sharding import PartitionSpec as P

H = 12
KV = 2
HD = 128

epsilon = 1e-06
rope_base = 1000000.0
neg_large = -1e30

bf16 = jnp.bfloat16
f32 = jnp.float32
VMEM_BYTES = 56 * 2**20

EVERY = ("grp", "core", "fsdp")
SEQ_AXES = ("grp", "core")
TP_AXES = ("fsdp", "core")


def rms_scale(values):
    return lax.rsqrt(jnp.mean(values * values, axis=-1, keepdims=True) + epsilon)


def rope_tables(places):
    half_width = HD // 2
    frequency = rope_base ** (-2.0 * jnp.arange(half_width, dtype=jnp.float32) / HD)
    angles = places.astype(jnp.float32)[:, None] * frequency[None, :]
    cosine, sine = jnp.cos(angles), jnp.sin(angles)
    return jnp.concatenate([cosine, cosine], axis=1), jnp.concatenate([-sine, sine], axis=1)


def matmul(left, right):
    return jnp.dot(left, right, preferred_element_type=jnp.float32)


def matmul_nt(left, right):
    return lax.dot_general(
        left, right, (((1,), (1,)), ((), ())), preferred_element_type=jnp.float32
    )


def inner(left, right):
    return lax.dot_general(
        left, right, (((0,), (0,)), ((), ())), preferred_element_type=jnp.float32
    )


def low(values):
    return values.astype(jnp.bfloat16)


def after(values, *others):
    return lax.optimization_barrier((values, others))[0]


def exchange(values, bit):
    count = lax.axis_size("grp")
    return lax.ppermute(values, "grp", [(i, i ^ bit) for i in range(count)])


def other_core(values):
    return lax.ppermute(values, "core", [(0, 1), (1, 0)])


def gather_group(block):
    count = lax.axis_size("grp")
    if count != 4:
        bit = 1
        while bit < count:
            block = jnp.concatenate([block, exchange(block, bit)], axis=0)
            bit *= 2
        return block
    half = block.shape[1] // 2
    from_x = exchange(block, 1)
    from_y = exchange(block, 2)
    left = exchange(from_x[:, :half], 2)
    right = exchange(from_y[:, half:], 1)
    corner = jnp.concatenate([left, right], axis=1)
    return jnp.concatenate([block, from_x, from_y, corner], axis=0)


def gather_near(block):
    return exchange(block, 1), exchange(block, 2)


def gather_far(block, near, *before):
    from_x, from_y = near
    half = block.shape[-1] // 2
    left = exchange(after(from_x, *before)[..., :half], 2)
    right = exchange(after(from_y, *before)[..., half:], 1)
    return block, from_x, from_y, left, right


def join(pieces):
    rows, width = pieces[0].shape
    spare = jnp.zeros((-rows % 16, width), bf16)
    corner = jnp.concatenate(pieces[3:], axis=1)
    slots = []
    for piece in (*pieces[:3], corner):
        slots += [piece, spare]
    return jnp.concatenate(slots, axis=0)


def scatter_group(parts, rows, *before):
    count = lax.axis_size("grp")
    slot = parts.shape[0] // count
    if count != 4:
        bit = count // 2
        parts = parts.astype(jnp.float32)
        while bit:
            keep, give = parts[: bit * rows], parts[bit * rows :]
            parts = keep + exchange(low(give), bit).astype(jnp.float32)
            bit //= 2
        return after(parts, *before)
    half = parts.shape[1] // 2
    own, for_x, for_y, corner = (
        parts[i * slot : i * slot + rows].astype(jnp.float32) for i in range(4)
    )
    corner = low(corner)
    from_x = exchange(corner[:, :half], 1).astype(jnp.float32)
    from_y = exchange(corner[:, half:], 2).astype(jnp.float32)
    for_y = jnp.concatenate([for_y[:, :half] + from_x, for_y[:, half:]], axis=1)
    for_x = jnp.concatenate([for_x[:, :half], for_x[:, half:] + from_y], axis=1)
    from_x = exchange(after(low(for_x), *before), 1).astype(jnp.float32)
    from_y = exchange(after(low(for_y), *before), 2).astype(jnp.float32)
    return own + from_x + from_y


def gather_chips(block):
    return [block] + [exchange(block, step) for step in range(1, lax.axis_size("grp"))]


def gather_small(block):
    mine = gather_chips(block)
    return mine + [other_core(piece) for piece in mine]


def plane_spots(pieces):
    if len(pieces) > lax.axis_size("grp"):
        return (0, 0), (1, 0), (2, 0), (3, 0), (3, pieces[3].shape[1])
    return tuple((i, 0) for i in range(len(pieces)))


def gather_plane(block, *before):
    part = block.shape[1] // 2
    if lax.axis_size("grp") != 4 or part < 512:
        return gather_chips(block)
    from_x, from_y = gather_near(block)
    left = exchange(after(from_x, *before)[:, :part], 2)
    right = exchange(after(from_y, *before)[:, part:], 1)
    return [block, from_x, from_y, left, right]


def gather_rows(block, *before):
    return lax.all_gather(after(block, *before), ("core", "fsdp"), axis=0, tiled=True)


def weight_near(rows):
    half = rows.shape[1] // 2
    own = lax.dynamic_slice_in_dim(rows, lax.axis_index("core") * half, half, 1)
    return (own, *gather_near(own)) if lax.axis_size("grp") == 4 else (own,)


def gather_weight(rows, near, before=(), late=()):
    count = lax.axis_size("grp")
    height, half = rows.shape[0], rows.shape[1] // 2
    if count == 4:
        part = half // 2
        own, from_x, from_y = near
        left = exchange(after(from_x, *before)[:, :part], 2)
        right = exchange(after(from_y, *before)[:, part:], 1)
        spots = ((1, 0), (2, 0), (3, 0), (3, part))
        mine = (from_x, from_y, left, right)
        other = tuple(other_core(piece) for piece in mine[:2])
        other += tuple(other_core(after(piece, *late)) for piece in mine[2:])
        return spots, rows, mine, other
    else:
        blocks = gather_group(near[0])
        spots = tuple((i, 0) for i in range(1, count))
        mine = tuple(blocks[i * height : (i + 1) * height] for i in range(1, count))
    return spots, rows, mine, tuple(other_core(piece) for piece in mine)


def gather_stacked(pieces, *before):
    stack = after(jnp.stack(pieces), *before)
    return (), lax.all_gather(stack, ("core", "fsdp"), axis=0, tiled=False), (), ()


def assemble(spots, own_ref, mine_refs, other_refs, full_ref, sems):
    grp, core = lax.axis_index("grp"), lax.axis_index("core")
    if len(own_ref.shape) == 4:
        count = own_ref.shape[1]
        copies = [
            pltpu.make_async_copy(own_ref.at[:, i], full_ref.at[grp ^ i], sems.at[i])
            for i in range(count)
        ]
        for copy in copies:
            copy.start()
        return copies
    height, half = own_ref.shape[0], full_ref.shape[1] // 2

    def rows_of(step):
        return pl.ds(pl.multiple_of((grp ^ step) * height, height), height)

    copies = [pltpu.make_async_copy(own_ref, full_ref.at[rows_of(0), :], sems.at[0])]
    for place, (step, offset) in enumerate(spots):
        for side, refs in ((core, mine_refs), (1 - core, other_refs)):
            width = refs[place].shape[1]
            start = pl.multiple_of(side * half + offset, 128)
            copies.append(
                pltpu.make_async_copy(
                    refs[place],
                    full_ref.at[rows_of(step), pl.ds(start, width)],
                    sems.at[len(copies)],
                )
            )
    for copy in copies:
        copy.start()
    return copies


def call(kernel, outs, ins, anys=(), scratch=()):
    whole = pl.BlockSpec(memory_space=pltpu.VMEM)
    left = pl.BlockSpec(memory_space=pl.ANY)
    return pl.pallas_call(
        kernel,
        out_shape=[jax.ShapeDtypeStruct(shape, dtype) for shape, dtype in outs],
        in_specs=[whole] * len(ins) + [left] * len(anys),
        out_specs=[whole] * len(outs),
        scratch_shapes=list(scratch),
        compiler_params=pltpu.CompilerParams(vmem_limit_bytes=VMEM_BYTES),
    )(*ins, *anys)


def weight_scratch(gathered, shape):
    spots, own, mine, other = gathered
    if len(own.shape) == 4:
        parts, count, rows, width = own.shape
        return [
            pltpu.VMEM((count, parts, rows, width), bf16),
            pltpu.SemaphoreType.DMA((count,)),
        ]
    return [
        pltpu.VMEM(shape, bf16),
        pltpu.SemaphoreType.DMA((1 + 2 * len(mine),)),
    ]


def weight_args(gathered):
    spots, own, mine, other = gathered
    return [own, *mine, *other]


def weight_refs(gathered, refs):
    count = len(gathered[2])
    return gathered[0], refs[0], refs[1 : 1 + count], refs[1 + count : 1 + 2 * count]


def rope(values, cosine, sine):
    return values * cosine + pltpu.roll(values, HD // 2, 1) * sine


def half_span(run, rows):
    return slice(run * rows // 2, (run + 1) * rows // 2)


def run_span(run, head, heads, rows):
    start = (run * H + head) * (rows // 2)
    return slice(start, start + heads * (rows // 2))


def project_kernel(gathered, refs):
    hidden, gain, bias, cosine, sine = refs[:5]
    count = 1 + 2 * len(gathered[2])
    pieces = refs[5 : 5 + count]
    normed, queries, pairs, weight, sems = refs[5 + count :]
    copies = assemble(*weight_refs(gathered, pieces), weight, sems)
    inputs = hidden[...].astype(f32)
    normed[...] = low(inputs * rms_scale(inputs) * gain[...])
    for copy in copies:
        copy.wait()
    rows = hidden.shape[0]
    half = weight.shape[1] // 2
    heads_half = half // HD
    for side in range(2):
        lin = (
            matmul(normed[...], weight[:, side * half : (side + 1) * half])
            + bias[:, side * half : (side + 1) * half]
        )
        for spot in range(heads_half):
            head = side * heads_half + spot
            part = lin[:, spot * HD : (spot + 1) * HD]
            if head < H + KV:
                part = rope(part, cosine[...], sine[...])
            if head < H:
                for run in range(2):
                    queries[run_span(run, head, 1, rows), :] = low(part)[half_span(run, rows)]
            else:
                pairs[:, (head - H) * HD : (head - H + 1) * HD] = low(part)


def fetch_pairs(refs, full_ref, sems):
    half = refs[0].shape[0] // 2
    copies = []
    for run in range(2):
        for i, ref in enumerate(refs):
            place = run * len(refs) + i
            copies.append(
                pltpu.make_async_copy(
                    ref.at[pl.ds(run * half, half), :],
                    full_ref.at[pl.ds(place * half, half), :],
                    sems.at[place],
                )
            )
    for copy in copies:
        copy.start()
    return copies


def allowed_keys(run, key_places, own_places):
    extent = key_places.shape[1] // 2 * (run + 1)
    own = own_places[half_span(run, own_places.shape[0]), :]
    own = jnp.concatenate([own] * (H // KV), axis=0)
    return extent, key_places[:, :extent] <= own


def attend_kernel(blocks, refs):
    queries, key_places, own_places = refs[:3]
    pair_refs = refs[3 : 3 + blocks]
    mixed, log_sums, pairs, pair_sems = refs[3 + blocks :]
    for copy in fetch_pairs(pair_refs, pairs, pair_sems):
        copy.wait()
    rows = own_places.shape[0]
    half = rows // 2
    scale = HD ** (-0.5)
    group_size = H // KV
    for run in range(2):
        extent, allowed = allowed_keys(run, key_places, own_places)
        for group in range(KV):
            keys = pairs[:extent, group * HD : (group + 1) * HD]
            values = pairs[:extent, (KV + group) * HD : (KV + group + 1) * HD]
            span = run_span(run, group * group_size, group_size, rows)
            scores = jnp.where(allowed, matmul_nt(queries[span, :], keys) * scale, neg_large)
            top = jnp.max(scores, axis=1, keepdims=True)
            terms = jnp.exp(scores - top)
            total = jnp.sum(terms, axis=1, keepdims=True)
            log_sums[span, :] = top + jnp.log(total)
            result = low(matmul(low(terms * (1.0 / total)), values))
            for spot in range(group_size):
                head = group * group_size + spot
                mixed[half_span(run, rows), head * HD : (head + 1) * HD] = result[
                    spot * half : (spot + 1) * half
                ]


def output_kernel(gathered, refs):
    mixed, hidden, gain = refs[:3]
    count = 1 + 2 * len(gathered[2])
    pieces = refs[3 : 3 + count]
    middle, normed_two, weight, sems = refs[3 + count :]
    for copy in assemble(*weight_refs(gathered, pieces), weight, sems):
        copy.wait()
    full = weight[...].reshape(mixed.shape[1], -1)
    result = hidden[...].astype(f32) + matmul(mixed[...], full)
    middle[...] = result
    normed_two[...] = low(result * rms_scale(result) * gain[...])


def norm_back(delta, values, gain):
    scale = rms_scale(values)
    unit = values * scale
    scaled = delta * gain
    return scale * (scaled - unit * jnp.mean(scaled * unit, axis=-1, keepdims=True)), unit


def middle_kernel(gathered, refs):
    normed_delta, middle, cotangent, gain = refs[:4]
    count = 1 + 2 * len(gathered[2])
    pieces = refs[4 : 4 + count]
    middle_delta, attention_low, mixed_delta, gain_part, weight, sems = refs[4 + count :]
    copies = assemble(*weight_refs(gathered, pieces), weight, sems)
    delta = normed_delta[...].astype(f32)
    term, unit = norm_back(delta, middle[...], gain[...])
    gain_part[...] = jnp.sum(delta * unit, axis=0, keepdims=True)
    result = cotangent[...].astype(f32) + term
    middle_delta[...] = result
    attention_low[...] = low(result)
    for copy in copies:
        copy.wait()
    rows = middle.shape[0]
    mixed = matmul_nt(low(result), weight[...].reshape(-1, result.shape[1]))
    for head in range(H):
        part = low(mixed[:, head * HD : (head + 1) * HD])
        for run in range(2):
            mixed_delta[run_span(run, head, 1, rows), :] = part[half_span(run, rows)]


def attend_back_kernel(blocks, refs):
    queries, mixed_delta, log_sums, key_places, own_places, cosine, sine, attention_low = refs[:8]
    pair_refs = refs[8 : 8 + blocks]
    deltas, bias_part, pair_mine, pair_other, pairs, pair_sems = refs[8 + blocks :]
    split = attention_low.shape[1]
    deltas[:, :split] = attention_low[...]
    for copy in fetch_pairs(pair_refs, pairs, pair_sems):
        copy.wait()
    rows = own_places.shape[0]
    half = rows // 2
    scale = HD ** (-0.5)
    group_size = H // KV
    for group in range(KV):
        key_span = slice(group * HD, (group + 1) * HD)
        value_span = slice((KV + group) * HD, (KV + group + 1) * HD)
        sums = []
        for run in range(2):
            extent, allowed = allowed_keys(run, key_places, own_places)
            keys, values = pairs[:extent, key_span], pairs[:extent, value_span]
            span = run_span(run, group * group_size, group_size, rows)
            query, mixed = queries[span, :], mixed_delta[span, :]
            scores = matmul_nt(query, keys) * scale
            probs = jnp.where(allowed, jnp.exp(scores - log_sums[span, :]), 0.0)
            prob_delta = matmul_nt(mixed, values)
            dots = jnp.sum(probs * prob_delta, axis=1, keepdims=True)
            score_delta = low(probs * (prob_delta - dots))
            turn = matmul(score_delta, keys) * scale
            here = half_span(run, rows)
            for spot in range(group_size):
                head = group * group_size + spot
                head_span = slice(head * HD, (head + 1) * HD)
                part = turn[spot * half : (spot + 1) * half]
                part = low(rope(part, cosine[here, :], sine[here, :]))
                deltas[here, split + head * HD : split + (head + 1) * HD] = part
                bias = jnp.sum(part.astype(f32), axis=0, keepdims=True)
                bias_part[:, head_span] = bias if run == 0 else bias_part[:, head_span] + bias
            sums.append((inner(score_delta, query) * scale, inner(low(probs), mixed)))
        early = sums[1][0].shape[0] // 2
        for which, to in enumerate((key_span, value_span)):
            first = sums[0][which] + sums[1][which][:early]
            for run, part in enumerate((first, sums[1][which][early:])):
                for block in range(blocks):
                    piece = part[block * half : (block + 1) * half]
                    start = block % (blocks // 2) * rows + run * half
                    if block < blocks // 2:
                        pair_mine[start : start + half, to] = piece
                    else:
                        pair_other[start : start + half, to] = low(piece)


def pair_split_kernel(refs):
    mine, received, own = refs[:3]
    rows = own.shape[0]
    own[...] = mine[:rows] + received[:rows].astype(f32)
    for place, part in enumerate(refs[3:], 1):
        span = slice(place * rows, (place + 1) * rows)
        part[...] = low(mine[span] + received[span].astype(f32))


def pair_sum_kernel(parts, refs):
    own = refs[0]
    cosine, sine, pair_delta, bias_part = refs[1 + parts :]
    total = own[...]
    for part in refs[1 : 1 + parts]:
        total = total + part[...].astype(f32)
    for spot in range(2 * KV):
        span = slice(spot * HD, (spot + 1) * HD)
        part = total[:, span]
        if spot < KV:
            part = rope(part, cosine[...], sine[...])
        part = low(part)
        pair_delta[:, span] = part
        bias_part[:, span] = jnp.sum(part.astype(f32), axis=0, keepdims=True)


def weight_grad_kernel(places, split, refs):
    mixed, unit = refs[:2]
    pieces = refs[2 : 2 + len(places)]
    result, deltas, sems = refs[2 + len(places) :]
    grp = lax.axis_index("grp")
    copies = []
    for place, piece in enumerate(pieces):
        step, start = places[place]
        rows, width = piece.shape
        row = pl.multiple_of((grp ^ step) * rows, rows)
        copies.append(
            pltpu.make_async_copy(
                piece, deltas.at[pl.ds(row, rows), pl.ds(start, width)], sems.at[place]
            )
        )
    for copy in copies:
        copy.start()
    for copy in copies:
        copy.wait()
    parts = low(inner(mixed[...], deltas[:, :split])), low(inner(unit[...], deltas[:, split:]))
    cores, devices = 2, lax.axis_size("fsdp")
    rows = result.shape[0] // (cores * devices)
    if rows % 16:
        result[:, :split], result[:, split:] = parts
        return
    for device in range(devices):
        for core in range(cores):
            here = (device * cores + core) * rows
            there = (core * devices + device) * rows
            for part, span in zip(parts, (slice(0, split), slice(split, None))):
                result[here : here + rows, span] = part[there : there + rows]


def weight_grad(mixed, unit, split, *gathered):
    places, pieces, start = [], [], 0
    for group in gathered:
        places += [(step, start + offset) for step, offset in plane_spots(group)]
        pieces += group
        start += group[0].shape[1]
    (part,) = call(
        lambda *refs: weight_grad_kernel(places, split, refs),
        [((unit.shape[1], start), bf16)],
        [mixed, unit],
        pieces,
        [pltpu.VMEM((unit.shape[0], start), bf16), pltpu.SemaphoreType.DMA((len(pieces),))],
    )
    return part


def forward_back_kernel(count, refs):
    normed, active_delta = refs[:2]
    pieces = refs[2 : 2 + 2 * (count + 1)]
    active, deltas, normed_delta, weights, sems = refs[2 + 2 * (count + 1) :]
    rows, width = pieces[0].shape
    slot = weights.shape[1] // count

    @pl.when(pl.program_id(0) == 0)
    def fetch():
        copies = []
        for which in range(2):
            for place in range(count + 1):
                piece = pieces[which * (count + 1) + place]
                step = min(place, count - 1)
                start = width // 2 if place == count else 0
                copies.append(
                    pltpu.make_async_copy(
                        piece,
                        weights.at[which, pl.ds(step * slot, rows), pl.ds(start, piece.shape[1])],
                        sems.at[len(copies)],
                    )
                )
        for copy in copies:
            copy.start()
        for copy in copies:
            copy.wait()
        if slot > rows:
            for which in range(2):
                for step in range(count):
                    spare = slice(step * slot + rows, (step + 1) * slot)
                    weights[which, spare, :] = jnp.zeros((slot - rows, width), bf16)

    gate = matmul_nt(normed[...], weights[0])
    upward = matmul_nt(normed[...], weights[1])
    delta = active_delta[...].astype(f32)
    sigmoid = 1.0 / (1.0 + jnp.exp(-gate))
    silu = gate * sigmoid
    active[0] = low(silu * upward)
    gate_low = low(delta * upward * (sigmoid * (1.0 + gate * (1.0 - sigmoid))))
    up_low = low(delta * silu)
    deltas[0] = gate_low
    deltas[1] = up_low
    normed_delta[...] = low(matmul(gate_low, weights[0]) + matmul(up_low, weights[1]))


def forward_back(normed_all, active_delta, pieces):
    tokens, width = normed_all.shape
    units = active_delta.shape[1]
    tile = 256

    def tiles(columns):
        return pl.BlockSpec((tile, columns), lambda i: (i, 0))

    count = len(pieces) // 2 - 1
    return pl.pallas_call(
        lambda *refs: forward_back_kernel(count, refs),
        grid=(tokens // tile,),
        out_shape=[
            jax.ShapeDtypeStruct((1, tokens, units), bf16),
            jax.ShapeDtypeStruct((2, tokens, units), bf16),
            jax.ShapeDtypeStruct((tokens, width), bf16),
        ],
        in_specs=[tiles(width), tiles(units)] + [pl.BlockSpec(memory_space=pl.ANY)] * len(pieces),
        out_specs=[
            pl.BlockSpec((1, tile, units), lambda i: (0, i, 0)),
            pl.BlockSpec((2, tile, units), lambda i: (0, i, 0)),
            tiles(width),
        ],
        scratch_shapes=[
            pltpu.VMEM((2, units, width), bf16),
            pltpu.SemaphoreType.DMA((len(pieces),)),
        ],
        compiler_params=pltpu.CompilerParams(vmem_limit_bytes=VMEM_BYTES),
    )(normed_all, active_delta, *pieces)


def outer_kernel(refs):
    left, right, own, for_x, for_y, far_left, far_right = refs
    rows = own.shape[1]
    slot = left.shape[2] // 4
    total = inner(left[0], right[...])
    for place, part in enumerate((own, for_x, for_y)):
        part[0] = low(total[place * slot : place * slot + rows])
    far = low(total[3 * slot : 3 * slot + rows])

    @pl.when(pl.program_id(1) == 0)
    def first():
        far_left[0] = far

    @pl.when(pl.program_id(1) == 1)
    def second():
        far_right[0] = far


def outer(left, right, rows):
    stack, tokens, units = left.shape
    half = right.shape[1] // 2
    wide = jax.ShapeDtypeStruct((stack, rows, 2 * half), bf16)
    narrow = jax.ShapeDtypeStruct((stack, rows, half), bf16)
    by_half = pl.BlockSpec((1, rows, half), lambda i, j: (i, 0, j))
    whole = pl.BlockSpec((1, rows, half), lambda i, j: (i, 0, 0))
    return pl.pallas_call(
        lambda *refs: outer_kernel(refs),
        grid=(stack, 2),
        out_shape=[wide, wide, wide, narrow, narrow],
        in_specs=[
            pl.BlockSpec((1, tokens, units), lambda i, j: (i, 0, 0)),
            pl.BlockSpec((tokens, half), lambda i, j: (0, j)),
        ],
        out_specs=[by_half, by_half, by_half, whole, whole],
        compiler_params=pltpu.CompilerParams(vmem_limit_bytes=VMEM_BYTES),
    )(left, right)


def scatter_far(parts):
    own, for_x, for_y, far_left, far_right = parts
    from_x = exchange(far_left, 1)
    from_y = exchange(far_right, 2)
    spare = jnp.zeros_like(from_x)
    to_y = low(for_y.astype(f32) + jnp.concatenate([from_x, spare], axis=2).astype(f32))
    to_x = low(for_x.astype(f32) + jnp.concatenate([spare, from_y], axis=2).astype(f32))
    return to_x, to_y


def scatter_near(own, from_x, from_y, late):
    from_x, from_y = after((from_x, from_y), late)
    return own.astype(f32) + from_x.astype(f32) + from_y.astype(f32)


def finish_kernel(gathered, refs):
    deltas, pair_delta, hidden, middle_delta, gain = refs[:5]
    count = 1 + 2 * len(gathered[2])
    pieces = refs[5 : 5 + count]
    input_delta, weight, sems = refs[5 + count :]
    copies = assemble(*weight_refs(gathered, pieces), weight, sems)
    for copy in copies:
        copy.wait()
    split = weight.shape[1] - pair_delta.shape[1]
    delta = matmul_nt(deltas[:, -split:], weight[:, :split]) + matmul_nt(
        pair_delta[...], weight[:, split:]
    )
    term, unit = norm_back(delta, hidden[...].astype(f32), gain[...])
    input_delta[...] = middle_delta[...] + term


def sum_over(values, *axes):
    for axis in axes:
        count = lax.axis_size(axis)
        bit = 1
        while bit < count:
            values = values + lax.ppermute(values, axis, [(i, i ^ bit) for i in range(count)])
            bit *= 2
    return values


def local(
    hidden,
    positions,
    first_gain,
    query_weight,
    key_weight,
    value_weight,
    query_bias,
    key_bias,
    value_bias,
    output_weight,
    second_gain,
    gate_weight,
    up_weight,
    down_weight,
    cotangent,
):
    rows = hidden.shape[0]
    width = hidden.shape[1]
    ctx_here = lax.axis_index("grp") * lax.axis_size("core") + lax.axis_index("core")
    own_places = lax.dynamic_slice_in_dim(positions, ctx_here * rows, rows)
    q_width, k_width = H * HD, KV * HD

    near = lax.axis_size("grp") == 4 and gate_weight.shape[1] % 8 == 0
    projections = jnp.concatenate([query_weight, key_weight, value_weight], axis=1)
    qkv_rows = gather_rows(projections)

    def columns(values):
        return lax.all_to_all(values, "grp", split_axis=1, concat_axis=0, tiled=True)

    inputs = hidden.astype(f32)
    unit = low(inputs * rms_scale(inputs))
    gate_own, up_own = gate_weight.T, up_weight.T
    small = jnp.concatenate([first_gain, second_gain, query_bias, key_bias, value_bias])
    devices = lax.axis_size(EVERY)
    device_here = lax.axis_index(EVERY)
    small_plane = sum_over(
        lax.dynamic_update_slice_in_dim(
            jnp.zeros((devices, small.shape[0]), jnp.float32),
            small.astype(jnp.float32)[None],
            device_here,
            0,
        ),
        "grp",
    )
    output_chips = gather_chips(output_weight)
    small_all = sum_over(small_plane, "core", "fsdp")
    down_near = gather_near(after(down_weight, small_plane, *output_chips[1:])) if near else ()
    down_pieces = gather_far(down_weight, down_near, small_all) if near else ()
    qkv_rows = after(qkv_rows, small_all, *down_near)
    qkv_near = weight_near(qkv_rows)
    own = width // devices
    kv_own = k_width // devices
    gain_one = small_all[:, :own].reshape(1, width)
    gain_two = small_all[:, own : 2 * own].reshape(1, width)
    bias_qkv = jnp.concatenate(
        [
            small_all[:, 2 * own : 3 * own].reshape(q_width),
            small_all[:, 3 * own : 3 * own + kv_own].reshape(k_width),
            small_all[:, 3 * own + kv_own :].reshape(k_width),
        ]
    ).reshape(1, -1)
    cotangent_all = lax.all_gather(cotangent, TP_AXES, axis=0, tiled=True)

    cosine, sine = rope_tables(own_places)
    places = positions.reshape(-1, rows)
    steps = jnp.arange(places.shape[0], dtype=jnp.int32)
    from_ctx = ctx_here ^ jnp.concatenate([steps[0::2], steps[1::2]])
    matches = from_ctx[:, None] == steps[None, :]
    key_places = jnp.sum(jnp.where(matches[:, :, None], places[None], 0), axis=1)
    key_places = key_places.reshape(-1, 2, rows // 2).transpose(1, 0, 2).reshape(1, -1)
    unit_columns = columns(unit)
    ready = (unit_columns, gain_one, gain_two, bias_qkv, cosine, sine, key_places)
    weight_qkv = gather_weight(qkv_rows, qkv_near, ready)
    if output_weight.shape[0] % 16:
        output_rows = gather_rows(output_weight, qkv_rows)
        weight_output = gather_weight(output_rows, weight_near(output_rows))
    else:
        weight_output = gather_stacked(output_chips, qkv_rows)

    normed, queries, pairs_local = call(
        lambda *refs: project_kernel(weight_qkv, refs),
        [((rows, width), bf16), ((H * rows, HD), bf16), ((rows, 2 * k_width), bf16)],
        [hidden, gain_one, bias_qkv, cosine, sine],
        weight_args(weight_qkv),
        weight_scratch(weight_qkv, (width, q_width + 2 * k_width)),
    )
    pairs = gather_small(pairs_local)
    blocks = len(pairs)
    length = blocks * rows
    query_places = own_places.reshape(rows, 1)
    pair_scratch = [
        pltpu.VMEM((length, 2 * k_width), bf16),
        pltpu.SemaphoreType.DMA((2 * blocks,)),
    ]
    mixed_low, log_sums = call(
        lambda *refs: attend_kernel(blocks, refs),
        [((rows, q_width), bf16), ((H * rows, 1), f32)],
        [queries, key_places, query_places],
        pairs,
        pair_scratch,
    )
    arrived = pairs[1 : blocks // 2]
    gate_near = gather_near(after(gate_own, *arrived)) if near else ()
    up_near = gather_near(after(up_own, *gate_near)) if near else ()
    middle, normed_two = call(
        lambda *refs: output_kernel(weight_output, refs),
        [((rows, width), f32), ((rows, width), bf16)],
        [mixed_low, hidden, gain_two],
        weight_args(weight_output),
        weight_scratch(weight_output, (q_width, width)),
    )
    normed_two = after(normed_two, *gate_near)


    normed_all = lax.all_gather(normed_two, TP_AXES, axis=0, tiled=True)
    if near:
        down_rows = join(down_pieces)
    else:
        down_rows = gather_group(down_weight)
    active_delta = low(matmul_nt(cotangent_all, down_rows))
    if near:
        active, unit_deltas, normed_two_part = forward_back(
            normed_all,
            active_delta,
            gather_far(gate_own, gate_near) + gather_far(up_own, up_near),
        )
    else:
        gate_rows, up_rows = gather_group(gate_own), gather_group(up_own)
        gate = matmul_nt(normed_all, gate_rows)
        upward = matmul_nt(normed_all, up_rows)
        delta = active_delta.astype(f32)
        sigmoid = 1.0 / (1.0 + jnp.exp(-gate))
        silu = gate * sigmoid
        active = low(silu * upward)
        gate_delta = low(delta * upward * (sigmoid * (1.0 + gate * (1.0 - sigmoid))))
        up_delta = low(delta * silu)
        normed_two_part = low(matmul(gate_delta, gate_rows) + matmul(up_delta, up_rows))
    normed_two_delta = lax.psum_scatter(
        normed_two_part, TP_AXES, scatter_dimension=0, tiled=True
    )
    mixed_columns = columns(after(mixed_low, normed_two_part))
    unit_rows = down_weight.shape[0]
    if near:
        down_parts = outer(active, cotangent_all, unit_rows)
        down_to = scatter_far(down_parts)
        both_parts = outer(after(unit_deltas, down_parts[0]), normed_all, unit_rows)
        both_to = scatter_far(both_parts)
        active = after(active[0], down_parts[0])
    out_part = matmul(active, down_rows)
    if near:
        normed_two_delta = after(normed_two_delta, both_parts[0], out_part, *down_to)
    out_sum = lax.psum_scatter(low(out_part), TP_AXES, scatter_dimension=0, tiled=True)

    middle_delta, attention_low, mixed_delta, second_gain_part = call(
        lambda *refs: middle_kernel(weight_output, refs),
        [
            ((rows, width), f32),
            ((rows, width), bf16),
            ((H * rows, HD), bf16),
            ((1, width), f32),
        ],
        [normed_two_delta, middle, cotangent, gain_two],
        weight_args(weight_output),
        weight_scratch(weight_output, (q_width, width)),
    )
    deltas, query_bias_part, pair_mine, pair_other = call(
        lambda *refs: attend_back_kernel(blocks, refs),
        [
            ((rows, width + q_width), bf16),
            ((1, q_width), f32),
            ((length // 2, 2 * k_width), f32),
            ((length // 2, 2 * k_width), bf16),
        ],
        [
            queries,
            mixed_delta,
            log_sums,
            key_places,
            query_places,
            cosine,
            -sine,
            attention_low,
        ],
        pairs,
        pair_scratch,
    )
    if near:
        down_from = exchange(down_to[0], 1), exchange(down_to[1], 2)
        pair_mine = after(pair_mine, *both_to, *down_from)
    cuts = call(
        lambda *refs: pair_split_kernel(refs),
        [((rows, 2 * k_width), f32)] + [((rows, 2 * k_width), bf16)] * (blocks // 2 - 1),
        [pair_mine, other_core(pair_other)],
    )
    pair_delta, pair_bias_part = call(
        lambda *refs: pair_sum_kernel(blocks // 2 - 1, refs),
        [((rows, 2 * k_width), bf16), ((1, 2 * k_width), f32)],
        [cuts[0]] + [exchange(cut, i) for i, cut in enumerate(cuts[1:], 1)] + [cosine, -sine],
    )
    small_plane = sum_over(
        jnp.concatenate([second_gain_part, query_bias_part, pair_bias_part], axis=1), "grp"
    )
    delta_pieces, pair_pieces = gather_plane(deltas, pair_delta), gather_chips(pair_delta)
    grad_part = weight_grad(mixed_columns, unit_columns, width, delta_pieces, pair_pieces)
    order = ("core", "fsdp") if output_weight.shape[0] % 16 else TP_AXES
    grads = lax.psum_scatter(grad_part, order, scatter_dimension=0, tiled=True).astype(f32)
    output_grad, unit_grad = grads[:, :width], grads[:, width:]
    (input_delta,) = call(
        lambda *refs: finish_kernel(weight_qkv, refs),
        [((rows, width), f32)],
        [deltas, pair_delta, hidden, middle_delta, gain_one],
        weight_args(weight_qkv),
        weight_scratch(weight_qkv, (width, q_width + 2 * k_width)),
    )
    first_gain_grad = jnp.sum(unit_grad * projections.astype(f32), axis=1)
    scaled_grad = unit_grad * first_gain.astype(f32)[:, None]

    if near:
        both_to = after(both_to, *delta_pieces, *pair_pieces, small_plane)
        both_from = exchange(both_to[0], 1), exchange(both_to[1], 2)
        down_grad = scatter_near(down_parts[0], *down_from, scaled_grad)[0]
        both_grads = scatter_near(both_parts[0], *both_from, (scaled_grad, first_gain_grad))
        gate_grad, up_grad = both_grads[0].T, both_grads[1].T
    else:
        down_grad = scatter_group(inner(active, cotangent_all), unit_rows)
        gate_grad = scatter_group(inner(gate_delta, normed_all), unit_rows).T
        up_grad = scatter_group(inner(up_delta, normed_all), unit_rows).T
    layer_out = low(middle + after(out_sum, pair_delta).astype(f32))

    small_sum = sum_over(small_plane, "core", "fsdp")[0]

    def own_part(start, size):
        return lax.dynamic_slice_in_dim(small_sum, start + device_here * size, size)

    return (
        layer_out,
        input_delta,
        first_gain_grad,
        scaled_grad[:, :q_width],
        scaled_grad[:, q_width : q_width + k_width],
        scaled_grad[:, q_width + k_width :],
        own_part(width, own),
        own_part(width + q_width, kv_own),
        own_part(width + q_width + k_width, kv_own),
        output_grad,
        own_part(0, own),
        gate_grad,
        up_grad,
        down_grad,
    )


def solution(mesh):
    cores = 2
    ctx, fsdp = mesh.shape["ctx"], mesh.shape["fsdp"]
    split = Mesh(mesh.devices.reshape(ctx // cores, cores, fsdp), EVERY)
    tokens = P(("fsdp", "grp", "core"), None)
    in_specs = (
        tokens,
        P("fsdp"),
        P(EVERY),
        P(EVERY, None),
        P(EVERY, None),
        P(EVERY, None),
        P(EVERY),
        P(EVERY),
        P(EVERY),
        P(EVERY, None),
        P(EVERY),
        P(None, EVERY),
        P(None, EVERY),
        P(EVERY, None),
        tokens,
    )
    out_specs = (
        tokens,
        tokens,
        P(EVERY),
        P(EVERY, None),
        P(EVERY, None),
        P(EVERY, None),
        P(EVERY),
        P(EVERY),
        P(EVERY),
        P(EVERY, None),
        P(EVERY),
        P(None, EVERY),
        P(None, EVERY),
        P(EVERY, None),
    )
    return jax.shard_map(local, mesh=split, in_specs=in_specs, out_specs=out_specs, check_vma=False)
```

profile of v0, /device:TPU:0, one launch (start us, length us, event | category | flops | bytes accessed | tf_op | source)
XLA Modules:
  0.0 385.0 jit_solution(14531252188593309547)
XLA Ops:
  12.5 3.0 collective-permute-start
  15.6 2.0 collective-permute-start.6
  20.7 3.5 collective-permute-done.1
  31.1 4.2 %collective-permute-done.3 = f32[32,160]{1,0:T(8,128)S(1)} collective-permute-done((f32[32,160]{1,0:T(8,128)S(1)}, f32[32,160]{1,0:T(8,128)S(1)}, u32[]{:S(2)}, u32[]{:S(2)}) %collective-permute-start.3) | collective-permute-done | bytes 20512 | tf_op jit(solution)/shard_map/ppermute | solution.py:678
  36.7 3.4 collective-permute-done.4
  40.2 1.8 pad_maximum_fusion
  42.0 3.2 collective-permute-done.8
  48.9 3.6 all-to-all-start
  54.2 2.1 collective-permute-start.10
  61.6 12.3 %collective-permute-done.10.refs_6_ = bf16[384,1024]{1,0:T(8,128)(2,1)S(1)} collective-permute-done((bf16[384,1024]{1,0:T(8,128)(2,1)S(1)}, bf16[384,1024]{1,0:T(8,128)(2,1)S(1)}, u32[]{:S(2)}, u32[]{:S(2)}) %collective-permute-start.10) | collective-permute-done | bytes 786464 | tf_op jit(solution)/shard_map/ppermute | solution.py:64
  77.3 6.0 %collective-permute-done.12.refs_8_ = bf16[384,512]{1,0:T(8,128)(2,1)S(1)} collective-permute-done((bf16[384,512]{1,0:T(8,128)(2,1)S(1)}, bf16[384,512]{1,0:T(8,128)(2,1)S(1)}, u32[]{:S(2)}, u32[]{:S(2)}) %collective-permute-start.12) | collective-permute-done | bytes 393248 | tf_op jit(solution)/shard_map/ppermute | solution.py:64
  83.3 4.7 %collective-permute-done.13.refs_9_ = bf16[384,512]{1,0:T(8,128)(2,1)S(1)} collective-permute-done((bf16[384,512]{1,0:T(8,128)(2,1)S(1)}, bf16[384,512]{1,0:T(8,128)(2,1)S(1)}, u32[]{:S(2)}, u32[]{:S(2)}) %collective-permute-start.13) | collective-permute-done | bytes 393248 | tf_op jit(solution)/shard_map/ppermute | solution.py:64
  90.5 5.7 %shard_map.254 = (bf16[128,1536]{1,0:T(8,128)(2,1)}, bf16[1536,128]{1,0:T(8,128)(2,1)}, bf16[128,512]{1,0:T(8,128)(2,1)}) custom-call(bf16[128,1536]{1,0:T(8,128)(2,1)} %refs_2_.3, f32[1,1536]{1,0:T(1,128)} %reshape.184.refs_1_.refs_4_, f32[1,2048]{1,0:T(1,128)} %bitcast.70, f32[128,128]{1,0:T(8,128)} %pad_maximum_fusion.1.refs_3_.refs_5_.refs_4_, ...), custom_call_target="tpu_custom_call" | custom-call | tf_op jit(solution)/shard_map/pallas_call | solution.py:231
  97.3 2.5 collective-permute-start.20
  99.8 3.1 collective-permute-done.18.refs_4_.refs_9_
  102.9 2.1 collective-permute-done.19.refs_5_.refs_10_
  110.7 6.1 %shard_map.255 = (bf16[128,1536]{1,0:T(8,128)(2,1)}, f32[1536,1]{1,0:T(8,128)}) custom-call(bf16[1536,128]{1,0:T(8,128)(2,1)} %get-tuple-element.75.refs_0_, s32[1,1024]{1,0:T(1,128)} %reshape.191.refs_1_.refs_3_, s32[128,1]{1,0:T(8,128)} %copy.48.refs_2_.refs_4_, bf16[128,512]{1,0:T(8,128)(2,1)} %get-tuple-element.76.refs_3_.refs_8_, ...), custom_call_target="tpu_custom_call" | custom-call | tf_op jit(solution)/shard_map/pallas_call | solution.py:231
  116.9 5.5 %shard_map.256 = (f32[128,1536]{1,0:T(8,128)}, bf16[128,1536]{1,0:T(8,128)(2,1)}) custom-call(bf16[128,1536]{1,0:T(8,128)(2,1)} %get-tuple-element.116.refs_0_, bf16[128,1536]{1,0:T(8,128)(2,1)} %refs_2_.3, f32[1,1536]{1,0:T(1,128)} %reshape.189.refs_2_.refs_3_, bf16[8,4,48,1536]{3,2,1,0:T(8,128)(2,1)} %bitcast.56), custom_call_target="tpu_custom_call" | custom-call | tf_op jit(solution)/shard_map/pallas_call | solution.py:231
  122.4 2.8 collective-permute-done.25.refs_3_
  132.8 8.5 %collective-permute-done.28 = bf16[280,768]{1,0:T(8,128)(2,1)S(1)} collective-permute-done((bf16[280,768]{1,0:T(8,128)(2,1)S(1)}, bf16[280,768]{1,0:T(8,128)(2,1)S(1)}, u32[]{:S(2)}, u32[]{:S(2)}) %collective-permute-start.28) | collective-permute-done | bytes 430112 | tf_op jit(solution)/shard_map/ppermute | solution.py:64
  144.2 15.5 %collective-permute-done.31.refs_8_ = bf16[280,1536]{1,0:T(8,128)(2,1)S(1)} collective-permute-done((bf16[280,1536]{1,0:T(8,128)(2,1)S(1)}, bf16[280,1536]{1,0:T(8,128)(2,1)S(1)}, u32[]{:S(2)}, u32[]{:S(2)}) %collective-permute-start.31) | collective-permute-done | bytes 860192 | tf_op jit(solution)/shard_map/ppermute | solution.py:64
  162.8 8.7 %fusion.refs_1_ = bf16[1024,1152]{1,0:T(8,128)(2,1)} fusion(bf16[1152,1536]{1,0:T(8,128)(2,1)} %copy-done.44, bf16[1024,1536]{1,0:T(8,128)(2,1)} %all-gather.10.cloned.1.call-done.refs_1_), kind=kOutput, calls=%fused_computation.4 | convolution fusion | flops 3625058304 | bytes 9043968 | tf_op jit(solution)/shard_map/dot_general | solution.py:43
  171.6 4.3 %collective-permute-done.33.refs_10_ = bf16[280,768]{1,0:T(8,128)(2,1)} collective-permute-done((bf16[280,768]{1,0:T(8,128)(2,1)S(1)}, bf16[280,768]{1,0:T(8,128)(2,1)}, u32[]{:S(2)}, u32[]{:S(2)}) %collective-permute-start.33) | collective-permute-done | bytes 430112 | tf_op jit(solution)/shard_map/ppermute | solution.py:64
  177.6 23.4 %shard_map.257 = (bf16[1,1024,1152]{2,1,0:T(8,128)(2,1)}, bf16[2,1024,1152]{2,1,0:T(8,128)(2,1)}, bf16[1024,1536]{1,0:T(8,128)(2,1)}) custom-call(bf16[1024,1536]{1,0:T(8,128)(2,1)} %all-gather.8.cloned.1.call-done.refs_0_.refs_1_, bf16[1024,1152]{1,0:T(8,128)(2,1)} %fusion.refs_1_, bf16[280,1536]{1,0:T(8,128)(2,1)} %bitcast.17.refs_2_, ...), custom_call_target="tpu_custom_call" | custom-call | tf_op jit(solution)/shard_map/pallas_call | solution.py:582
  201.0 8.0 %shard_map.258 = (bf16[1,280,1536]{2,1,0:T(8,128)(2,1)}, bf16[1,280,1536]{2,1,0:T(8,128)(2,1)}, bf16[1,280,1536]{2,1,0:T(8,128)(2,1)}, bf16[1,280,768]{2,1,0:T(8,128)(2,1)}, bf16[1,280,768]{2,1,0:T(8,128)(2,1)}) custom-call(bf16[1,1024,1152]{2,1,0:T(8,128)(2,1)} %get-tuple-element.86.refs_0_, bf16[1024,1536]{1,0:T(8,128)(2,1)} %all-gather.10.cloned.1.call-done.refs_1_), custom_call_target="tpu_custom_call" | custom-call | tf_op jit(solution)/shard_map/pallas_call | solution.py:629
  209.0 7.6 %fusion.13 = bf16[1024,1536]{1,0:T(8,128)(2,1)} fusion(bf16[1024,1152]{1,0:T(8,128)(2,1)S(1)} %bitcast.58, bf16[1152,1536]{1,0:T(8,128)(2,1)} %copy-done.44), kind=kOutput, calls=%fused_computation.62 | convolution fusion | flops 3623878656 | bytes 9043968 | tf_op jit(solution)/shard_map/dot_general | solution.py:39
  220.6 12.5 %shard_map.259 = (bf16[2,280,1536]{2,1,0:T(8,128)(2,1)}, bf16[2,280,1536]{2,1,0:T(8,128)(2,1)}, bf16[2,280,1536]{2,1,0:T(8,128)(2,1)}, bf16[2,280,768]{2,1,0:T(8,128)(2,1)}, bf16[2,280,768]{2,1,0:T(8,128)(2,1)}) custom-call(bf16[2,1024,1152]{2,1,0:T(8,128)(2,1)} %get-tuple-element.91.refs_0_, bf16[1024,1536]{1,0:T(8,128)(2,1)} %all-gather.8.cloned.1.call-done.refs_0_.refs_1_), custom_call_target="tpu_custom_call" | custom-call | tf_op jit(solution)/shard_map/pallas_call | solution.py:629
  240.3 6.1 %shard_map.260 = (f32[128,1536]{1,0:T(8,128)}, bf16[128,1536]{1,0:T(8,128)(2,1)}, bf16[1536,128]{1,0:T(8,128)(2,1)}, f32[1,1536]{1,0:T(1,128)}) custom-call(bf16[128,1536]{1,0:T(8,128)(2,1)} %reduce-scatter.6.cloned.1.call-done.refs_0_, f32[128,1536]{1,0:T(8,128)} %get-tuple-element.79.refs_1_, bf16[128,1536]{1,0:T(8,128)(2,1)} %refs_2_.2, ...), custom_call_target="tpu_custom_call" | custom-call | tf_op jit(solution)/shard_map/pallas_call | solution.py:231
  246.5 9.2 %shard_map.261 = (bf16[128,3072]{1,0:T(8,128)(2,1)}, f32[1,1536]{1,0:T(1,128)}, f32[512,512]{1,0:T(8,128)}, bf16[512,512]{1,0:T(8,128)(2,1)}) custom-call(bf16[1536,128]{1,0:T(8,128)(2,1)} %get-tuple-element.75.refs_0_, bf16[1536,128]{1,0:T(8,128)(2,1)} %get-tuple-element.98.refs_1_, f32[1536,1]{1,0:T(8,128)} %get-tuple-element.99.refs_2_, ...), custom_call_target="tpu_custom_call" | custom-call | tf_op jit(solution)/shard_map/pallas_call | solution.py:231
  260.2 2.7 add_convert_fusion
  262.9 11.5 %collective-permute-done.39 = bf16[1,280,1536]{2,1,0:T(8,128)(2,1)} collective-permute-done((bf16[1,280,1536]{2,1,0:T(8,128)(2,1)}, bf16[1,280,1536]{2,1,0:T(8,128)(2,1)}, u32[]{:S(2)}, u32[]{:S(2)}) %collective-permute-start.39) | collective-permute-done | bytes 860192 | tf_op jit(solution)/shard_map/ppermute | solution.py:64
  275.2 2.2 shard_map.262
  280.9 12.9 %collective-permute-done.42.refs_1_ = bf16[128,512]{1,0:T(8,128)(2,1)S(1)} collective-permute-done((bf16[128,512]{1,0:T(8,128)(2,1)}, bf16[128,512]{1,0:T(8,128)(2,1)S(1)}, u32[]{:S(2)}, u32[]{:S(2)}) %collective-permute-start.42) | collective-permute-done | bytes 131104 | tf_op jit(solution)/shard_map/ppermute | solution.py:64
  293.8 2.3 collective-permute-done.44.refs_3_
  296.7 1.9 shard_map.263
  302.3 4.1 %all-to-all-start.1 = ((bf16[128,4,384]{2,0,1:T(8,128)(2,1)}), bf16[128,4,384]{2,0,1:T(8,128)(2,1)}, u32[]{:S(2)}, u32[]{:S(2)}) async-start(bf16[128,4,384]{2,0,1:T(8,128)(2,1)} %bitcast.61), calls=%async_computation.3 | async-start | bytes 786432 | tf_op jit(solution)/shard_map/all_to_all | solution.py:711
  310.3 6.8 %all-to-all-done.1 = bf16[128,4,384]{2,0,1:T(8,128)(2,1)} async-done(((bf16[128,4,384]{2,0,1:T(8,128)(2,1)}), bf16[128,4,384]{2,0,1:T(8,128)(2,1)}, u32[]{:S(2)}, u32[]{:S(2)}) %all-to-all-start.1) | async-done | bytes 393248 | tf_op jit(solution)/shard_map/all_to_all | solution.py:711
  318.5 2.4 collective-permute-done.51.refs_10_
  320.9 6.3 %shard_map.265 = bf16[384,3584]{1,0:T(8,128)(2,1)} custom-call(bf16[512,384]{1,0:T(8,128)(2,1)} %bitcast.22.refs_0_, bf16[512,384]{1,0:T(8,128)(2,1)} %bitcast.59, bf16[128,3072]{1,0:T(8,128)(2,1)} %get-tuple-element.114.refs_0_.refs_2_, bf16[128,3072]{1,0:T(8,128)(2,1)} %copy-done.16, bf16[128,3072]{1,0:T(8,128)(2,1)} %copy-done.17, ...), custom_call_target="tpu_custom_call" | custom-call | tf_op jit(solution)/shard_map/pallas_call | solution.py:231
  328.6 2.5 collective-permute-done.52
  331.8 3.3 collective-permute-done.53
  338.3 3.7 collective-permute-done.55
  343.2 1.8 add_convert_fusion.4
  345.0 7.7 %shard_map.264 = f32[128,1536]{1,0:T(8,128)} custom-call(bf16[128,3072]{1,0:T(8,128)(2,1)} %get-tuple-element.114.refs_0_.refs_2_, bf16[128,512]{1,0:T(8,128)(2,1)} %get-tuple-element.112.refs_1_.refs_7_, bf16[128,1536]{1,0:T(8,128)(2,1)} %refs_2_.3, f32[128,1536]{1,0:T(8,128)} %get-tuple-element.115.refs_3_, f32[1,1536]{1,0:T(1,128)} %reshape.184.refs_1_.refs_4_, ...), custom_call_target="tpu_custom_call" | custom-call | tf_op jit(solution)/shard_map/pallas_call | solution.py:231
  354.0 9.1 %reduce-scatter.8.cloned.1.call-done = bf16[48,3584]{1,0:T(8,128)(2,1)} async-done(((bf16[384,3584]{1,0:T(8,128)(2,1)}), bf16[48,3584]{1,0:T(8,128)(2,1)}) %reduce-scatter.8.cloned.1.call-update) | async-done | bytes 344080 | tf_op jit(solution)/shard_map/reduce_scatter | solution.py:889
  367.2 2.1 collective-permute-done.57
  370.8 2.6 convert_add_fusion
  373.5 3.9 %slice_bitcast_fusion = (f32[1536,280]{0,1:T(8,128)}, f32[1536,280]{0,1:T(8,128)}, f32[280,1536]{1,0:T(8,128)}) fusion(f32[2,280,1536]{2,1,0:T(8,128)S(1)} %convert_add_fusion, bf16[1,280,1536]{2,1,0:T(8,128)(2,1)} %collective-permute-done.40, bf16[1,280,1536]{2,1,0:T(8,128)(2,1)} %collective-permute-done.39, bf16[1,280,1536]{2,1,0:T(8,128)(2,1)S(1)} %copy-done.32), kind=kLoop, calls=%fused_computation.5 | loop fusion | flops 2150400 | bytes 11182080 | tf_op jit(solution)/shard_map/transpose | solution.py:906
  (308 shorter events, 98.7 us)
Async XLA Ops:
  7.2 39.8 %all-gather.6.cloned.1.call-start = ((), (), s32[]{:S(2)}) async-start(), calls=%async_computation.5 | async-start | bytes 1769472 | tf_op jit(solution)/shard_map/all_gather | solution.py:161
  11.6 105.3 %all-gather.12.cloned.1.call-start = ((), (), s32[]{:S(2)}) async-start(), calls=%async_computation.11 | async-start | bytes 5308416 | tf_op jit(solution)/shard_map/all_gather | solution.py:192
  15.5 8.7 %collective-permute-start.5 = (bf16[48,1536]{1,0:T(8,128)(2,1)}, bf16[48,1536]{1,0:T(8,128)(2,1)S(1)}, u32[]{:S(2)}, u32[]{:S(2)}) collective-permute-start(bf16[48,1536]{1,0:T(8,128)(2,1)} %param.24), channel_id=1, source_target_pairs={{0,8},{8,0},{16,24},{24,16},{1,9},{9,1},{17,25},{25,17},{2,10},{10... | collective-permute-start | bytes 442376 | tf_op jit(solution)/shard_map/ppermute | solution.py:64
  25.2 19.9 %collective-permute-start.8 = (bf16[280,1536]{1,0:T(8,128)(2,1)}, bf16[280,1536]{1,0:T(8,128)(2,1)S(1)}, u32[]{:S(2)}, u32[]{:S(2)}) collective-permute-start(bf16[280,1536]{1,0:T(8,128)(2,1)} %param.28), channel_id=1, source_target_pairs={{0,8},{8,0},{16,24},{24,16},{1,9},{9,1},{17,25},{25,17},{2,10},{10... | collective-permute-start | bytes 2580488 | tf_op jit(solution)/shard_map/ppermute | solution.py:64
  26.8 19.4 %collective-permute-start.9 = (bf16[280,1536]{1,0:T(8,128)(2,1)}, bf16[280,1536]{1,0:T(8,128)(2,1)S(1)}, u32[]{:S(2)}, u32[]{:S(2)}) collective-permute-start(bf16[280,1536]{1,0:T(8,128)(2,1)} %param.28), channel_id=1, source_target_pairs={{0,16},{8,24},{16,0},{24,8},{1,17},{9,25},{17,1},{25,9},{2,18},{10... | collective-permute-start | bytes 2580488 | tf_op jit(solution)/shard_map/ppermute | solution.py:64
  47.1 115.8 %all-gather.10.cloned.1.call-start = ((), (), s32[]{:S(2)}) async-start(), calls=%async_computation.7 | async-start | bytes 3538944 | tf_op jit(solution)/shard_map/all_gather | solution.py:745
  48.9 12.7 %all-to-all-start = ((bf16[128,4,384]{2,0,1:T(8,128)(2,1)}), bf16[128,4,384]{2,0,1:T(8,128)(2,1)S(1)}, u32[]{:S(2)}, u32[]{:S(2)}) async-start(bf16[128,4,384]{2,0,1:T(8,128)(2,1)} %bitcast.55), calls=%async_computation | async-start | bytes 786432 | tf_op jit(solution)/shard_map/all_to_all | solution.py:711
  52.5 125.1 %all-gather.8.cloned.1.call-start = ((), (), s32[]{:S(2)}) async-start(), calls=%async_computation.6 | async-start | bytes 3538944 | tf_op jit(solution)/shard_map/all_gather | solution.py:798
  54.2 19.7 %collective-permute-start.10 = (bf16[384,1024]{1,0:T(8,128)(2,1)S(1)}, bf16[384,1024]{1,0:T(8,128)(2,1)S(1)}, u32[]{:S(2)}, u32[]{:S(2)}) collective-permute-start(bf16[384,1024]{1,0:T(8,128)(2,1)S(1)} %constant_dynamic-slice_fusion.4), channel_id=1, source_target_pairs={{0,8},{8,0},{16,24},{24,16},{1,9},{9,1},{17,25},{25,17},{2,10},{10... | collective-permute-start | bytes 2359304 | tf_op jit(solution)/shard_map/ppermute | solution.py:64
  56.3 20.0 %collective-permute-start.11 = (bf16[384,1024]{1,0:T(8,128)(2,1)S(1)}, bf16[384,1024]{1,0:T(8,128)(2,1)S(1)}, u32[]{:S(2)}, u32[]{:S(2)}) collective-permute-start(bf16[384,1024]{1,0:T(8,128)(2,1)S(1)} %constant_dynamic-slice_fusion.4), channel_id=1, source_target_pairs={{0,16},{8,24},{16,0},{24,8},{1,17},{9,25},{17,1},{25,9},{2,18},{10... | collective-permute-start | bytes 2359304 | tf_op jit(solution)/shard_map/ppermute | solution.py:64
  74.0 9.3 %collective-permute-start.12 = (bf16[384,512]{1,0:T(8,128)(2,1)S(1)}, bf16[384,512]{1,0:T(8,128)(2,1)S(1)}, u32[]{:S(2)}, u32[]{:S(2)}) collective-permute-start(bf16[384,512]{1,0:T(8,128)(2,1)S(1)} %slice.79), channel_id=1, source_target_pairs={{0,16},{8,24},{16,0},{24,8},{1,17},{9,25},{17,1},{25,9},{2,18},{10... | collective-permute-start | bytes 1179656 | tf_op jit(solution)/shard_map/ppermute | solution.py:64
  76.3 11.7 %collective-permute-start.14 = (bf16[384,1024]{1,0:T(8,128)(2,1)S(1)}, bf16[384,1024]{1,0:T(8,128)(2,1)S(1)}, u32[]{:S(2)}, u32[]{:S(2)}) collective-permute-start(bf16[384,1024]{1,0:T(8,128)(2,1)S(1)} %collective-permute-done.10.refs_6_), channel_id=1, source_target_pairs={{0,4},{4,0},{1,5},{5,1},{2,6},{6,2},{3,7},{7,3},{8,12},{12,8},{9,1... | collective-permute-start | bytes 2359304 | tf_op jit(solution)/shard_map/ppermute | solution.py:68
  76.4 11.6 %collective-permute-start.15 = (bf16[384,1024]{1,0:T(8,128)(2,1)S(1)}, bf16[384,1024]{1,0:T(8,128)(2,1)S(1)}, u32[]{:S(2)}, u32[]{:S(2)}) collective-permute-start(bf16[384,1024]{1,0:T(8,128)(2,1)S(1)} %collective-permute-done.11.refs_7_), channel_id=1, source_target_pairs={{0,4},{4,0},{1,5},{5,1},{2,6},{6,2},{3,7},{7,3},{8,12},{12,8},{9,1... | collective-permute-start | bytes 2359304 | tf_op jit(solution)/shard_map/ppermute | solution.py:68
  76.9 11.1 %collective-permute-start.13 = (bf16[384,512]{1,0:T(8,128)(2,1)S(1)}, bf16[384,512]{1,0:T(8,128)(2,1)S(1)}, u32[]{:S(2)}, u32[]{:S(2)}) collective-permute-start(bf16[384,512]{1,0:T(8,128)(2,1)S(1)} %slice.80), channel_id=1, source_target_pairs={{0,8},{8,0},{16,24},{24,16},{1,9},{9,1},{17,25},{25,17},{2,10},{10... | collective-permute-start | bytes 1179656 | tf_op jit(solution)/shard_map/ppermute | solution.py:64
  105.0 20.2 %collective-permute-start.25 = (bf16[280,1536]{1,0:T(8,128)(2,1)}, bf16[280,1536]{1,0:T(8,128)(2,1)S(1)}, u32[]{:S(2)}, u32[]{:S(2)}) collective-permute-start(bf16[280,1536]{1,0:T(8,128)(2,1)} %bitcast.17.refs_2_), channel_id=1, source_target_pairs={{0,8},{8,0},{16,24},{24,16},{1,9},{9,1},{17,25},{25,17},{2,10},{10... | collective-permute-start | bytes 2580488 | tf_op jit(solution)/shard_map/ppermute | solution.py:64
  106.7 20.0 %collective-permute-start.26 = (bf16[280,1536]{1,0:T(8,128)(2,1)}, bf16[280,1536]{1,0:T(8,128)(2,1)S(1)}, u32[]{:S(2)}, u32[]{:S(2)}) collective-permute-start(bf16[280,1536]{1,0:T(8,128)(2,1)} %bitcast.17.refs_2_), channel_id=1, source_target_pairs={{0,16},{8,24},{16,0},{24,8},{1,17},{9,25},{17,1},{25,9},{2,18},{10... | collective-permute-start | bytes 2580488 | tf_op jit(solution)/shard_map/ppermute | solution.py:64
  126.7 113.6 %reduce-scatter.6.cloned.1.call-start = ((), (), s32[]{:S(2)}) async-start(), calls=%async_computation.9 | async-start | bytes 3538944 | tf_op jit(solution)/shard_map/reduce_scatter | solution.py:821
  128.3 12.9 %collective-permute-start.28 = (bf16[280,768]{1,0:T(8,128)(2,1)S(1)}, bf16[280,768]{1,0:T(8,128)(2,1)S(1)}, u32[]{:S(2)}, u32[]{:S(2)}) collective-permute-start(bf16[280,768]{1,0:T(8,128)(2,1)S(1)} %slice.82), channel_id=1, source_target_pairs={{0,8},{8,0},{16,24},{24,16},{1,9},{9,1},{17,25},{25,17},{2,10},{10... | collective-permute-start | bytes 1290248 | tf_op jit(solution)/shard_map/ppermute | solution.py:64
  129.0 12.9 %collective-permute-start.27 = (bf16[280,768]{1,0:T(8,128)(2,1)S(1)}, bf16[280,768]{1,0:T(8,128)(2,1)S(1)}, u32[]{:S(2)}, u32[]{:S(2)}) collective-permute-start(bf16[280,768]{1,0:T(8,128)(2,1)S(1)} %slice.81), channel_id=1, source_target_pairs={{0,16},{8,24},{16,0},{24,8},{1,17},{9,25},{17,1},{25,9},{2,18},{10... | collective-permute-start | bytes 1290248 | tf_op jit(solution)/shard_map/ppermute | solution.py:64
  130.5 29.2 %collective-permute-start.31 = (bf16[280,1536]{1,0:T(8,128)(2,1)S(1)}, bf16[280,1536]{1,0:T(8,128)(2,1)S(1)}, u32[]{:S(2)}, u32[]{:S(2)}) collective-permute-start(bf16[280,1536]{1,0:T(8,128)(2,1)S(1)} %bitcast.64), channel_id=1, source_target_pairs={{0,8},{8,0},{16,24},{24,16},{1,9},{9,1},{17,25},{25,17},{2,10},{10... | collective-permute-start | bytes 2580488 | tf_op jit(solution)/shard_map/ppermute | solution.py:64
  131.2 29.2 %collective-permute-start.32 = (bf16[280,1536]{1,0:T(8,128)(2,1)S(1)}, bf16[280,1536]{1,0:T(8,128)(2,1)S(1)}, u32[]{:S(2)}, u32[]{:S(2)}) collective-permute-start(bf16[280,1536]{1,0:T(8,128)(2,1)S(1)} %bitcast.65), channel_id=1, source_target_pairs={{0,16},{8,24},{16,0},{24,8},{1,17},{9,25},{17,1},{25,9},{2,18},{10... | collective-permute-start | bytes 2580488 | tf_op jit(solution)/shard_map/ppermute | solution.py:64
  142.1 29.5 %collective-permute-start.29 = (bf16[280,768]{1,0:T(8,128)(2,1)S(1)}, bf16[280,768]{1,0:T(8,128)(2,1)S(1)}, u32[]{:S(2)}, u32[]{:S(2)}) collective-permute-start(bf16[280,768]{1,0:T(8,128)(2,1)S(1)} %slice.101), channel_id=1, source_target_pairs={{0,16},{8,24},{16,0},{24,8},{1,17},{9,25},{17,1},{25,9},{2,18},{10... | collective-permute-start | bytes 1290248 | tf_op jit(solution)/shard_map/ppermute | solution.py:64
  143.5 28.0 %collective-permute-start.30 = (bf16[280,768]{1,0:T(8,128)(2,1)S(1)}, bf16[280,768]{1,0:T(8,128)(2,1)S(1)}, u32[]{:S(2)}, u32[]{:S(2)}) collective-permute-start(bf16[280,768]{1,0:T(8,128)(2,1)S(1)} %slice.102), channel_id=1, source_target_pairs={{0,8},{8,0},{16,24},{24,16},{1,9},{9,1},{17,25},{25,17},{2,10},{10... | collective-permute-start | bytes 1290248 | tf_op jit(solution)/shard_map/ppermute | solution.py:64
  159.7 16.1 %collective-permute-start.33 = (bf16[280,768]{1,0:T(8,128)(2,1)S(1)}, bf16[280,768]{1,0:T(8,128)(2,1)}, u32[]{:S(2)}, u32[]{:S(2)}) collective-permute-start(bf16[280,768]{1,0:T(8,128)(2,1)S(1)} %slice.103), channel_id=1, source_target_pairs={{0,16},{8,24},{16,0},{24,8},{1,17},{9,25},{17,1},{25,9},{2,18},{10... | collective-permute-start | bytes 1290248 | tf_op jit(solution)/shard_map/ppermute | solution.py:64
  161.3 14.5 %collective-permute-start.34 = (bf16[280,768]{1,0:T(8,128)(2,1)S(1)}, bf16[280,768]{1,0:T(8,128)(2,1)}, u32[]{:S(2)}, u32[]{:S(2)}) collective-permute-start(bf16[280,768]{1,0:T(8,128)(2,1)S(1)} %slice.104), channel_id=1, source_target_pairs={{0,8},{8,0},{16,24},{24,16},{1,9},{9,1},{17,25},{25,17},{2,10},{10... | collective-permute-start | bytes 1290248 | tf_op jit(solution)/shard_map/ppermute | solution.py:64
  201.0 137.4 %reduce-scatter.4.cloned.1.call-start = ((), (), s32[]{:S(2)}) async-start(), calls=%async_computation.8 | async-start | bytes 3538944 | tf_op jit(solution)/shard_map/reduce_scatter | solution.py:835
  217.6 16.5 %collective-permute-start.35 = (bf16[1,280,768]{2,1,0:T(8,128)(2,1)S(1)}, bf16[1,280,768]{2,1,0:T(8,128)(2,1)S(1)}, u32[]{:S(2)}, u32[]{:S(2)}) collective-permute-start(bf16[1,280,768]{2,1,0:T(8,128)(2,1)S(1)} %copy-done.56), channel_id=1, source_target_pairs={{0,16},{8,24},{16,0},{24,8},{1,17},{9,25},{17,1},{25,9},{2,18},{10... | collective-permute-start | bytes 1290248 | tf_op jit(solution)/shard_map/ppermute | solution.py:64
  219.1 17.6 %collective-permute-start.36 = (bf16[1,280,768]{2,1,0:T(8,128)(2,1)S(1)}, bf16[1,280,768]{2,1,0:T(8,128)(2,1)S(1)}, u32[]{:S(2)}, u32[]{:S(2)}) collective-permute-start(bf16[1,280,768]{2,1,0:T(8,128)(2,1)S(1)} %copy-done.55), channel_id=1, source_target_pairs={{0,8},{8,0},{16,24},{24,16},{1,9},{9,1},{17,25},{25,17},{2,10},{10... | collective-permute-start | bytes 1290248 | tf_op jit(solution)/shard_map/ppermute | solution.py:64
  233.0 24.1 %collective-permute-start.37 = (bf16[2,280,768]{2,1,0:T(8,128)(2,1)}, bf16[2,280,768]{2,1,0:T(8,128)(2,1)S(1)}, u32[]{:S(2)}, u32[]{:S(2)}) collective-permute-start(bf16[2,280,768]{2,1,0:T(8,128)(2,1)} %get-tuple-element.103), channel_id=1, source_target_pairs={{0,16},{8,24},{16,0},{24,8},{1,17},{9,25},{17,1},{25,9},{2,18},{10... | collective-permute-start | bytes 2580488 | tf_op jit(solution)/shard_map/ppermute | solution.py:64
  233.6 26.5 %collective-permute-start.38 = (bf16[2,280,768]{2,1,0:T(8,128)(2,1)}, bf16[2,280,768]{2,1,0:T(8,128)(2,1)}, u32[]{:S(2)}, u32[]{:S(2)}) collective-permute-start(bf16[2,280,768]{2,1,0:T(8,128)(2,1)} %get-tuple-element.105), channel_id=1, source_target_pairs={{0,8},{8,0},{16,24},{24,16},{1,9},{9,1},{17,25},{25,17},{2,10},{10... | collective-permute-start | bytes 2580488 | tf_op jit(solution)/shard_map/ppermute | solution.py:64
  235.2 39.2 %collective-permute-start.39 = (bf16[1,280,1536]{2,1,0:T(8,128)(2,1)}, bf16[1,280,1536]{2,1,0:T(8,128)(2,1)}, u32[]{:S(2)}, u32[]{:S(2)}) collective-permute-start(bf16[1,280,1536]{2,1,0:T(8,128)(2,1)} %add_convert_fusion.3), channel_id=1, source_target_pairs={{0,8},{8,0},{16,24},{24,16},{1,9},{9,1},{17,25},{25,17},{2,10},{10... | collective-permute-start | bytes 2580488 | tf_op jit(solution)/shard_map/ppermute | solution.py:64
  237.8 36.6 %collective-permute-start.40 = (bf16[1,280,1536]{2,1,0:T(8,128)(2,1)}, bf16[1,280,1536]{2,1,0:T(8,128)(2,1)}, u32[]{:S(2)}, u32[]{:S(2)}) collective-permute-start(bf16[1,280,1536]{2,1,0:T(8,128)(2,1)} %add_convert_fusion.2), channel_id=1, source_target_pairs={{0,16},{8,24},{16,0},{24,8},{1,17},{9,25},{17,1},{25,9},{2,18},{10... | collective-permute-start | bytes 2580488 | tf_op jit(solution)/shard_map/ppermute | solution.py:64
  255.6 43.0 %collective-permute-start.45 = (bf16[128,3072]{1,0:T(8,128)(2,1)}, bf16[128,3072]{1,0:T(8,128)(2,1)S(1)}, u32[]{:S(2)}, u32[]{:S(2)}) collective-permute-start(bf16[128,3072]{1,0:T(8,128)(2,1)} %get-tuple-element.114.refs_0_.refs_2_), channel_id=1, source_target_pairs={{0,8},{8,0},{16,24},{24,16},{1,9},{9,1},{17,25},{25,17},{2,10},{10... | collective-permute-start | bytes 2359304 | tf_op jit(solution)/shard_map/ppermute | solution.py:64
  257.2 42.8 %collective-permute-start.46 = (bf16[128,3072]{1,0:T(8,128)(2,1)}, bf16[128,3072]{1,0:T(8,128)(2,1)S(1)}, u32[]{:S(2)}, u32[]{:S(2)}) collective-permute-start(bf16[128,3072]{1,0:T(8,128)(2,1)} %get-tuple-element.114.refs_0_.refs_2_), channel_id=1, source_target_pairs={{0,16},{8,24},{16,0},{24,8},{1,17},{9,25},{17,1},{25,9},{2,18},{10... | collective-permute-start | bytes 2359304 | tf_op jit(solution)/shard_map/ppermute | solution.py:64
  260.1 14.3 %collective-permute-start.41 = (bf16[512,512]{1,0:T(8,128)(2,1)S(1)}, bf16[512,512]{1,0:T(8,128)(2,1)S(1)}, u32[]{:S(2)}, u32[]{:S(2)}) collective-permute-start(bf16[512,512]{1,0:T(8,128)(2,1)S(1)} %copy-done.54), channel_id=1, source_target_pairs={{0,4},{4,0},{1,5},{5,1},{2,6},{6,2},{3,7},{7,3},{8,12},{12,8},{9,1... | collective-permute-start | bytes 1572872 | tf_op jit(solution)/shard_map/ppermute | solution.py:68
  277.4 16.4 %collective-permute-start.42 = (bf16[128,512]{1,0:T(8,128)(2,1)}, bf16[128,512]{1,0:T(8,128)(2,1)S(1)}, u32[]{:S(2)}, u32[]{:S(2)}) collective-permute-start(bf16[128,512]{1,0:T(8,128)(2,1)} %get-tuple-element.109), channel_id=1, source_target_pairs={{0,8},{8,0},{16,24},{24,16},{1,9},{9,1},{17,25},{25,17},{2,10},{10... | collective-permute-start | bytes 393224 | tf_op jit(solution)/shard_map/ppermute | solution.py:64
  278.0 15.8 %collective-permute-start.43 = (bf16[128,512]{1,0:T(8,128)(2,1)}, bf16[128,512]{1,0:T(8,128)(2,1)S(1)}, u32[]{:S(2)}, u32[]{:S(2)}) collective-permute-start(bf16[128,512]{1,0:T(8,128)(2,1)} %get-tuple-element.110), channel_id=1, source_target_pairs={{0,16},{8,24},{16,0},{24,8},{1,17},{9,25},{17,1},{25,9},{2,18},{10... | collective-permute-start | bytes 393224 | tf_op jit(solution)/shard_map/ppermute | solution.py:64
  279.4 16.7 %collective-permute-start.44 = (bf16[128,512]{1,0:T(8,128)(2,1)}, bf16[128,512]{1,0:T(8,128)(2,1)S(1)}, u32[]{:S(2)}, u32[]{:S(2)}) collective-permute-start(bf16[128,512]{1,0:T(8,128)(2,1)} %get-tuple-element.111), channel_id=1, source_target_pairs={{0,24},{8,16},{16,8},{24,0},{1,25},{9,17},{17,9},{25,1},{2,26},{10... | collective-permute-start | bytes 393224 | tf_op jit(solution)/shard_map/ppermute | solution.py:64
  299.4 21.4 %collective-permute-start.47 = (bf16[128,1536]{1,0:T(8,128)(2,1)}, bf16[128,1536]{1,0:T(8,128)(2,1)}, u32[]{:S(2)}, u32[]{:S(2)}) collective-permute-start(bf16[128,1536]{1,0:T(8,128)(2,1)} %slice.87), channel_id=1, source_target_pairs={{0,16},{8,24},{16,0},{24,8},{1,17},{9,25},{17,1},{25,9},{2,18},{10... | collective-permute-start | bytes 1179656 | tf_op jit(solution)/shard_map/ppermute | solution.py:64
  300.8 20.0 %collective-permute-start.48 = (bf16[128,1536]{1,0:T(8,128)(2,1)}, bf16[128,1536]{1,0:T(8,128)(2,1)}, u32[]{:S(2)}, u32[]{:S(2)}) collective-permute-start(bf16[128,1536]{1,0:T(8,128)(2,1)} %slice.88), channel_id=1, source_target_pairs={{0,8},{8,0},{16,24},{24,16},{1,9},{9,1},{17,25},{25,17},{2,10},{10... | collective-permute-start | bytes 1179656 | tf_op jit(solution)/shard_map/ppermute | solution.py:64
  302.3 14.9 %all-to-all-start.1 = ((bf16[128,4,384]{2,0,1:T(8,128)(2,1)}), bf16[128,4,384]{2,0,1:T(8,128)(2,1)}, u32[]{:S(2)}, u32[]{:S(2)}) async-start(bf16[128,4,384]{2,0,1:T(8,128)(2,1)} %bitcast.61), calls=%async_computation.3 | async-start | bytes 786432 | tf_op jit(solution)/shard_map/all_to_all | solution.py:711
  306.4 56.7 %reduce-scatter.8.cloned.1.call-start = ((), (), s32[]{:S(2)}) async-start(), calls=%async_computation.10 | async-start | bytes 3096576 | tf_op jit(solution)/shard_map/reduce_scatter | solution.py:889
  306.8 11.7 %collective-permute-start.49 = (bf16[128,512]{1,0:T(8,128)(2,1)S(1)}, bf16[128,512]{1,0:T(8,128)(2,1)S(1)}, u32[]{:S(2)}, u32[]{:S(2)}) collective-permute-start(bf16[128,512]{1,0:T(8,128)(2,1)S(1)} %copy-done.33), channel_id=1, source_target_pairs={{0,8},{8,0},{16,24},{24,16},{1,9},{9,1},{17,25},{25,17},{2,10},{10... | collective-permute-start | bytes 393224 | tf_op jit(solution)/shard_map/ppermute | solution.py:64
  308.4 10.0 %collective-permute-start.50 = (bf16[128,512]{1,0:T(8,128)(2,1)S(1)}, bf16[128,512]{1,0:T(8,128)(2,1)}, u32[]{:S(2)}, u32[]{:S(2)}) collective-permute-start(bf16[128,512]{1,0:T(8,128)(2,1)S(1)} %copy-done.33), channel_id=1, source_target_pairs={{0,16},{8,24},{16,0},{24,8},{1,17},{9,25},{17,1},{25,9},{2,18},{10... | collective-permute-start | bytes 393224 | tf_op jit(solution)/shard_map/ppermute | solution.py:64
  309.9 11.0 %collective-permute-start.51 = (bf16[128,512]{1,0:T(8,128)(2,1)S(1)}, bf16[128,512]{1,0:T(8,128)(2,1)}, u32[]{:S(2)}, u32[]{:S(2)}) collective-permute-start(bf16[128,512]{1,0:T(8,128)(2,1)S(1)} %copy-done.33), channel_id=1, source_target_pairs={{0,24},{8,16},{16,8},{24,0},{1,25},{9,17},{17,9},{25,1},{2,26},{10... | collective-permute-start | bytes 393224 | tf_op jit(solution)/shard_map/ppermute | solution.py:64
  335.1 34.2 %collective-permute-start.57 = (bf16[2,280,1536]{2,1,0:T(8,128)(2,1)S(1)}, bf16[2,280,1536]{2,1,0:T(8,128)(2,1)}, u32[]{:S(2)}, u32[]{:S(2)}) collective-permute-start(bf16[2,280,1536]{2,1,0:T(8,128)(2,1)S(1)} %add_convert_fusion.1), channel_id=1, source_target_pairs={{0,8},{8,0},{16,24},{24,16},{1,9},{9,1},{17,25},{25,17},{2,10},{10... | collective-permute-start | bytes 5160968 | tf_op jit(solution)/shard_map/ppermute | solution.py:64
  336.5 34.4 %collective-permute-start.58 = (bf16[2,280,1536]{2,1,0:T(8,128)(2,1)}, bf16[2,280,1536]{2,1,0:T(8,128)(2,1)}, u32[]{:S(2)}, u32[]{:S(2)}) collective-permute-start(bf16[2,280,1536]{2,1,0:T(8,128)(2,1)} %add_convert_fusion), channel_id=1, source_target_pairs={{0,16},{8,24},{16,0},{24,8},{1,17},{9,25},{17,1},{25,9},{2,18},{10... | collective-permute-start | bytes 5160968 | tf_op jit(solution)/shard_map/ppermute | solution.py:64
  342.1 10.7 %collective-permute-start.56 = (f32[1,3584]{1,0:T(1,128)S(1)}, f32[1,3584]{1,0:T(1,128)S(1)}, u32[]{:S(2)}, u32[]{:S(2)}) collective-permute-start(f32[1,3584]{1,0:T(1,128)S(1)} %add.140), channel_id=1, source_target_pairs={{0,2},{1,3},{2,0},{3,1},{4,6},{5,7},{6,4},{7,5},{8,10},{9,11},{10,... | collective-permute-start | bytes 43016 | tf_op jit(solution)/shard_map/ppermute | solution.py:678
  (77 other events, 663.2 us)
Sparse Core Ops, SparseCore 0:
  11.7 28.9 all-gather.5
  47.2 52.4 all-gather.11
  101.3 37.5 all-gather.9
  140.4 37.1 all-gather.7
  201.1 39.1 reduce-scatter.5
  242.5 39.4 reduce-scatter.3
  327.4 35.6 reduce-scatter.7
where the time goes:
time: 386 us; the launch traced here: 385 us
  waiting for transfers between devices  147 us (38%)
  Pallas kernels  94.6 us (25%)
  starting transfers between devices  66.7 us (17%)
  local copies, waits for them, and re-layouts  22.7 us (6%)
  other arithmetic  22.3 us (6%)
  matrix products  16.3 us (4%)
  between operations  15 us (4%)
    ppermute x40, waiting for transfers between devices, exchange(): return lax.ppermute(values, 'grp', [(i, i ^ bit) for i in range(count)])  102 us
    pallas_call x9, Pallas kernels, call(): pl.pallas_call(kernel, out_shape=[jax.ShapeDtypeStruct(shape, dtype) for...  50.8 us
    ppermute x40, starting transfers between devices, exchange(): return lax.ppermute(values, 'grp', [(i, i ^ bit) for i in range(count)])  46 us
    pallas_call x1, Pallas kernels, forward_back(): pl.pallas_call(lambda *refs: forward_back_kernel(count, refs), grid=(toke...  23.4 us
    ppermute x10, waiting for transfers between devices, sum_over(): lax.ppermute(values, axis, [(i, i ^ bit) for i in range(count)])  23 us
    pallas_call x2, Pallas kernels, outer(): pl.pallas_call(lambda *refs: outer_kernel(refs), grid=(stack, 2), out_sha...  20.4 us
    ppermute x10, starting transfers between devices, sum_over(): lax.ppermute(values, axis, [(i, i ^ bit) for i in range(count)])  11.1 us
    unnamed x124, local copies, waits for them, and re-layouts  10.2 us
  transfers between devices with their start and end apart: 68, of which 38 were waited for; matrix products, arithmetic and copies ran while one was open for 11% of the time, Pallas kernels for 18%

commit v1 on v0

--- a/solution.py
+++ b/solution.py
@@ -654,6 +654,27 @@
     return own.astype(f32) + from_x.astype(f32) + from_y.astype(f32)
 
 
+def turn_kernel(refs):
+    own, from_x, from_y = refs[:3]
+    for place, out in enumerate(refs[3:]):
+        total = own[place].astype(f32) + from_x[place].astype(f32) + from_y[place].astype(f32)
+        out[...] = total.T
+
+
+def turned_sums(own, from_x, from_y, late):
+    from_x, from_y = after((from_x, from_y), late)
+    stack, rows, width = own.shape
+    tile = width // 3 if width % 384 == 0 else width
+    return pl.pallas_call(
+        lambda *refs: turn_kernel(refs),
+        grid=(width // tile,),
+        out_shape=[jax.ShapeDtypeStruct((width, rows), f32)] * stack,
+        in_specs=[pl.BlockSpec((stack, rows, tile), lambda i: (0, 0, i))] * 3,
+        out_specs=[pl.BlockSpec((tile, rows), lambda i: (i, 0))] * stack,
+        compiler_params=pltpu.CompilerParams(vmem_limit_bytes=VMEM_BYTES),
+    )(own, from_x, from_y)
+
+
 def finish_kernel(gathered, refs):
     deltas, pair_delta, hidden, middle_delta, gain = refs[:5]
     count = 1 + 2 * len(gathered[2])
@@ -751,7 +772,7 @@
     matches = from_ctx[:, None] == steps[None, :]
     key_places = jnp.sum(jnp.where(matches[:, :, None], places[None], 0), axis=1)
     key_places = key_places.reshape(-1, 2, rows // 2).transpose(1, 0, 2).reshape(1, -1)
-    unit_columns = columns(unit)
+    unit_columns = columns(after(unit, qkv_near[0]))
     ready = (unit_columns, gain_one, gain_two, bias_qkv, cosine, sine, key_places)
     weight_qkv = gather_weight(qkv_rows, qkv_near, ready)
     if output_weight.shape[0] % 16:
@@ -796,6 +817,8 @@
 
 
     normed_all = lax.all_gather(normed_two, TP_AXES, axis=0, tiled=True)
+    mixed_columns = columns(after(mixed_low, normed_two))
+    normed_all = after(normed_all, mixed_columns)
     if near:
         down_rows = join(down_pieces)
     else:
@@ -821,7 +844,6 @@
     normed_two_delta = lax.psum_scatter(
         normed_two_part, TP_AXES, scatter_dimension=0, tiled=True
     )
-    mixed_columns = columns(after(mixed_low, normed_two_part))
     unit_rows = down_weight.shape[0]
     if near:
         down_parts = outer(active, cotangent_all, unit_rows)
@@ -868,8 +890,7 @@
         pair_scratch,
     )
     if near:
-        down_from = exchange(down_to[0], 1), exchange(down_to[1], 2)
-        pair_mine = after(pair_mine, *both_to, *down_from)
+        pair_mine = after(pair_mine, *both_to)
     cuts = call(
         lambda *refs: pair_split_kernel(refs),
         [((rows, 2 * k_width), f32)] + [((rows, 2 * k_width), bf16)] * (blocks // 2 - 1),
@@ -901,9 +922,10 @@
     if near:
         both_to = after(both_to, *delta_pieces, *pair_pieces, small_plane)
         both_from = exchange(both_to[0], 1), exchange(both_to[1], 2)
+        down_to = after(down_to, pair_delta)
+        down_from = exchange(down_to[0], 1), exchange(down_to[1], 2)
         down_grad = scatter_near(down_parts[0], *down_from, scaled_grad)[0]
-        both_grads = scatter_near(both_parts[0], *both_from, (scaled_grad, first_gain_grad))
-        gate_grad, up_grad = both_grads[0].T, both_grads[1].T
+        gate_grad, up_grad = turned_sums(both_parts[0], *both_from, (scaled_grad, first_gain_grad))
     else:
         down_grad = scatter_group(inner(active, cotangent_all), unit_rows)
         gate_grad = scatter_group(inner(gate_delta, normed_all), unit_rows).T

time: 386 us -> 381 us (0.987)
  waiting for transfers between devices: 147 us -> 137 us
  local copies, waits for them, and re-layouts: 22.7 us -> 28.3 us
  Pallas kernels: 94.6 us -> 100 us
  other arithmetic: 22.3 us -> 17.4 us
    ppermute x40, waiting for transfers between devices: 102 us -> 86 us  [exchange(): return lax.ppermute(values, 'grp', [(i, i ^ bit) for i in range(count)])]
    all_to_all x2, waiting for transfers between devices: 6.85 us -> 14.9 us  [columns(): lax.all_to_all(values, 'grp', split_axis=1, concat_axis=0, tiled=True)]
    pallas_call x0 -> x1, Pallas kernels: none -> 5.65 us  [turned_sums(): pl.pallas_call(lambda *refs: turn_kernel(refs), grid=(width // tile,), ou...]
    transpose x1 -> x0, other arithmetic: 3.91 us -> none  [local(): gate_grad, up_grad = (both_grads[0].T, both_grads[1].T)]
    unnamed x124 -> x120, local copies, waits for them, and re-layouts: 10.2 us -> 13.7 us
  transfers between devices with their start and end apart: 68 -> 68, of which waited for: 38 -> 35; matrix products, arithmetic and copies ran while one was open for 11% -> 13% of each run, Pallas kernels for 18% -> 20%
where the time goes in v1:
time: 381 us; the launch traced here: 380 us
  waiting for transfers between devices  137 us (36%)
  Pallas kernels  100 us (26%)
  starting transfers between devices  65.7 us (17%)
  local copies, waits for them, and re-layouts  28.3 us (7%)
  other arithmetic  17.4 us (5%)
  matrix products  16.3 us (4%)
  between operations  14.9 us (4%)
    ppermute x40, waiting for transfers between devices, exchange(): return lax.ppermute(values, 'grp', [(i, i ^ bit) for i in range(count)])  86 us
    pallas_call x9, Pallas kernels, call(): pl.pallas_call(kernel, out_shape=[jax.ShapeDtypeStruct(shape, dtype) for...  50.8 us
    ppermute x40, starting transfers between devices, exchange(): return lax.ppermute(values, 'grp', [(i, i ^ bit) for i in range(count)])  44.5 us
    pallas_call x1, Pallas kernels, forward_back(): pl.pallas_call(lambda *refs: forward_back_kernel(count, refs), grid=(toke...  23.4 us
    ppermute x10, waiting for transfers between devices, sum_over(): lax.ppermute(values, axis, [(i, i ^ bit) for i in range(count)])  21 us
    pallas_call x2, Pallas kernels, outer(): pl.pallas_call(lambda *refs: outer_kernel(refs), grid=(stack, 2), out_sha...  20.6 us
    all_to_all x2, waiting for transfers between devices, columns(): lax.all_to_all(values, 'grp', split_axis=1, concat_axis=0, tiled=True)  14.9 us
    unnamed x120, local copies, waits for them, and re-layouts  13.7 us
  transfers between devices with their start and end apart: 68, of which 35 were waited for; matrix products, arithmetic and copies ran while one was open for 13% of the time, Pallas kernels for 20%

profile of v1, /device:TPU:0, one launch (start us, length us, event | category | flops | bytes accessed | tf_op | source)
XLA Modules:
  0.0 379.9 jit_solution(6146639576833567926)
XLA Ops:
  11.3 3.0 collective-permute-start
  14.4 2.0 collective-permute-start.6
  19.5 3.5 collective-permute-done.1
  29.9 4.2 %collective-permute-done.3 = f32[32,160]{1,0:T(8,128)S(1)} collective-permute-done((f32[32,160]{1,0:T(8,128)S(1)}, f32[32,160]{1,0:T(8,128)S(1)}, u32[]{:S(2)}, u32[]{:S(2)}) %collective-permute-start.3) | collective-permute-done | bytes 20512 | tf_op jit(solution)/shard_map/ppermute | solution.py:699
  35.6 3.4 collective-permute-done.4
  39.0 1.8 pad_maximum_fusion
  40.8 3.2 collective-permute-done.8
  48.4 2.1 constant_dynamic-slice_fusion.4
  56.5 4.1 %all-to-all-start = ((bf16[128,4,384]{2,0,1:T(8,128)(2,1)}), bf16[128,4,384]{2,0,1:T(8,128)(2,1)}, u32[]{:S(2)}, u32[]{:S(2)}) async-start(bf16[128,4,384]{2,0,1:T(8,128)(2,1)} %bitcast.53), calls=%async_computation | async-start | bytes 786432 | tf_op jit(solution)/shard_map/all_to_all | solution.py:732
  62.3 10.5 %all-to-all-done = bf16[128,4,384]{2,0,1:T(8,128)(2,1)} async-done(((bf16[128,4,384]{2,0,1:T(8,128)(2,1)}), bf16[128,4,384]{2,0,1:T(8,128)(2,1)}, u32[]{:S(2)}, u32[]{:S(2)}) %all-to-all-start) | async-done | bytes 393248 | tf_op jit(solution)/shard_map/all_to_all | solution.py:732
  72.8 2.0 collective-permute-start.12
  76.9 3.8 %collective-permute-done.12.refs_8_ = bf16[384,512]{1,0:T(8,128)(2,1)S(1)} collective-permute-done((bf16[384,512]{1,0:T(8,128)(2,1)S(1)}, bf16[384,512]{1,0:T(8,128)(2,1)S(1)}, u32[]{:S(2)}, u32[]{:S(2)}) %collective-permute-start.12) | collective-permute-done | bytes 393248 | tf_op jit(solution)/shard_map/ppermute | solution.py:64
  80.8 2.0 collective-permute-done.13.refs_9_
  82.8 1.9 collective-permute-done.17.refs_13_
  85.5 5.7 %shard_map.254 = (bf16[128,1536]{1,0:T(8,128)(2,1)}, bf16[1536,128]{1,0:T(8,128)(2,1)}, bf16[128,512]{1,0:T(8,128)(2,1)}) custom-call(bf16[128,1536]{1,0:T(8,128)(2,1)} %refs_2_.3, f32[1,1536]{1,0:T(1,128)} %reshape.184.refs_1_.refs_4_, f32[1,2048]{1,0:T(1,128)} %bitcast.62, f32[128,128]{1,0:T(8,128)} %pad_maximum_fusion.1.refs_3_.refs_5_.refs_4_, ...), custom_call_target="tpu_custom_call" | custom-call | tf_op jit(solution)/shard_map/pallas_call | solution.py:231
  94.8 2.6 collective-permute-done.18.refs_4_.refs_9_
  97.3 3.6 collective-permute-done.19.refs_5_.refs_10_
  106.4 6.1 %shard_map.255 = (bf16[128,1536]{1,0:T(8,128)(2,1)}, f32[1536,1]{1,0:T(8,128)}) custom-call(bf16[1536,128]{1,0:T(8,128)(2,1)} %get-tuple-element.82.refs_0_, s32[1,1024]{1,0:T(1,128)} %reshape.191.refs_1_.refs_3_, s32[128,1]{1,0:T(8,128)} %copy.54.refs_2_.refs_4_, bf16[128,512]{1,0:T(8,128)(2,1)} %get-tuple-element.83.refs_3_.refs_8_, ...), custom_call_target="tpu_custom_call" | custom-call | tf_op jit(solution)/shard_map/pallas_call | solution.py:231
  112.6 5.5 %shard_map.256 = (f32[128,1536]{1,0:T(8,128)}, bf16[128,1536]{1,0:T(8,128)(2,1)}) custom-call(bf16[128,1536]{1,0:T(8,128)(2,1)} %get-tuple-element.90.refs_0_, bf16[128,1536]{1,0:T(8,128)(2,1)} %refs_2_.3, f32[1,1536]{1,0:T(1,128)} %reshape.189.refs_2_.refs_3_, bf16[8,4,48,1536]{3,2,1,0:T(8,128)(2,1)} %bitcast.48), custom_call_target="tpu_custom_call" | custom-call | tf_op jit(solution)/shard_map/pallas_call | solution.py:231
  118.1 3.2 collective-permute-done.25.refs_3_
  126.1 8.5 %collective-permute-done.28 = bf16[280,768]{1,0:T(8,128)(2,1)S(1)} collective-permute-done((bf16[280,768]{1,0:T(8,128)(2,1)S(1)}, bf16[280,768]{1,0:T(8,128)(2,1)S(1)}, u32[]{:S(2)}, u32[]{:S(2)}) %collective-permute-start.28) | collective-permute-done | bytes 430112 | tf_op jit(solution)/shard_map/ppermute | solution.py:64
  139.5 13.5 %collective-permute-done.31.refs_8_ = bf16[280,1536]{1,0:T(8,128)(2,1)S(1)} collective-permute-done((bf16[280,1536]{1,0:T(8,128)(2,1)S(1)}, bf16[280,1536]{1,0:T(8,128)(2,1)S(1)}, u32[]{:S(2)}, u32[]{:S(2)}) %collective-permute-start.31) | collective-permute-done | bytes 860192 | tf_op jit(solution)/shard_map/ppermute | solution.py:64
  157.0 3.5 all-to-all-start.1
  160.7 8.7 %fusion.refs_1_ = bf16[1024,1152]{1,0:T(8,128)(2,1)} fusion(bf16[1152,1536]{1,0:T(8,128)(2,1)} %copy-done.39, bf16[1024,1536]{1,0:T(8,128)(2,1)} %all-gather.10.cloned.1.call-done.refs_1_), kind=kOutput, calls=%fused_computation.3 | convolution fusion | flops 3625058304 | bytes 9043968 | tf_op jit(solution)/shard_map/dot_general | solution.py:43
  169.4 4.4 %all-to-all-done.1 = bf16[128,4,384]{2,0,1:T(8,128)(2,1)S(1)} async-done(((bf16[128,4,384]{2,0,1:T(8,128)(2,1)}), bf16[128,4,384]{2,0,1:T(8,128)(2,1)S(1)}, u32[]{:S(2)}, u32[]{:S(2)}) %all-to-all-start.1) | async-done | bytes 393248 | tf_op jit(solution)/shard_map/all_to_all | solution.py:732
  174.8 23.4 %shard_map.257 = (bf16[1,1024,1152]{2,1,0:T(8,128)(2,1)}, bf16[2,1024,1152]{2,1,0:T(8,128)(2,1)}, bf16[1024,1536]{1,0:T(8,128)(2,1)}) custom-call(bf16[1024,1536]{1,0:T(8,128)(2,1)} %all-gather.8.cloned.1.call-done.refs_0_.refs_1_, bf16[1024,1152]{1,0:T(8,128)(2,1)} %fusion.refs_1_, bf16[280,1536]{1,0:T(8,128)(2,1)} %bitcast.17.refs_2_, ...), custom_call_target="tpu_custom_call" | custom-call | tf_op jit(solution)/shard_map/pallas_call | solution.py:582
  198.3 8.0 %shard_map.258 = (bf16[1,280,1536]{2,1,0:T(8,128)(2,1)}, bf16[1,280,1536]{2,1,0:T(8,128)(2,1)}, bf16[1,280,1536]{2,1,0:T(8,128)(2,1)}, bf16[1,280,768]{2,1,0:T(8,128)(2,1)}, bf16[1,280,768]{2,1,0:T(8,128)(2,1)}) custom-call(bf16[1,1024,1152]{2,1,0:T(8,128)(2,1)} %get-tuple-element.95.refs_0_, bf16[1024,1536]{1,0:T(8,128)(2,1)} %all-gather.10.cloned.1.call-done.refs_1_), custom_call_target="tpu_custom_call" | custom-call | tf_op jit(solution)/shard_map/pallas_call | solution.py:629
  206.3 7.6 %fusion.13 = bf16[1024,1536]{1,0:T(8,128)(2,1)} fusion(bf16[1024,1152]{1,0:T(8,128)(2,1)S(1)} %bitcast.50, bf16[1152,1536]{1,0:T(8,128)(2,1)} %copy-done.39), kind=kOutput, calls=%fused_computation.59 | convolution fusion | flops 3623878656 | bytes 9043968 | tf_op jit(solution)/shard_map/dot_general | solution.py:39
  216.4 12.6 %shard_map.259 = (bf16[2,280,1536]{2,1,0:T(8,128)(2,1)}, bf16[2,280,1536]{2,1,0:T(8,128)(2,1)}, bf16[2,280,1536]{2,1,0:T(8,128)(2,1)}, bf16[2,280,768]{2,1,0:T(8,128)(2,1)}, bf16[2,280,768]{2,1,0:T(8,128)(2,1)}) custom-call(bf16[2,1024,1152]{2,1,0:T(8,128)(2,1)} %get-tuple-element.100.refs_0_, bf16[1024,1536]{1,0:T(8,128)(2,1)} %all-gather.8.cloned.1.call-done.refs_0_.refs_1_), custom_call_target="tpu_custom_call" | custom-call | tf_op jit(solution)/shard_map/pallas_call | solution.py:629
  232.8 9.1 %collective-permute-done.36 = bf16[1,280,768]{2,1,0:T(8,128)(2,1)S(1)} collective-permute-done((bf16[1,280,768]{2,1,0:T(8,128)(2,1)S(1)}, bf16[1,280,768]{2,1,0:T(8,128)(2,1)S(1)}, u32[]{:S(2)}, u32[]{:S(2)}) %collective-permute-start.36) | collective-permute-done | bytes 430112 | tf_op jit(solution)/shard_map/ppermute | solution.py:64
  243.0 6.4 %shard_map.260 = (f32[128,1536]{1,0:T(8,128)}, bf16[128,1536]{1,0:T(8,128)(2,1)}, bf16[1536,128]{1,0:T(8,128)(2,1)}, f32[1,1536]{1,0:T(1,128)}) custom-call(bf16[128,1536]{1,0:T(8,128)(2,1)} %reduce-scatter.6.cloned.1.call-done.refs_0_, f32[128,1536]{1,0:T(8,128)} %get-tuple-element.86.refs_1_, bf16[128,1536]{1,0:T(8,128)(2,1)} %refs_2_.2, ...), custom_call_target="tpu_custom_call" | custom-call | tf_op jit(solution)/shard_map/pallas_call | solution.py:231
  249.4 8.9 %shard_map.261 = (bf16[128,3072]{1,0:T(8,128)(2,1)}, f32[1,1536]{1,0:T(1,128)}, f32[512,512]{1,0:T(8,128)}, bf16[512,512]{1,0:T(8,128)(2,1)}) custom-call(bf16[1536,128]{1,0:T(8,128)(2,1)} %get-tuple-element.82.refs_0_, bf16[1536,128]{1,0:T(8,128)(2,1)} %get-tuple-element.107.refs_1_, f32[1536,1]{1,0:T(8,128)} %get-tuple-element.108.refs_2_, ...), custom_call_target="tpu_custom_call" | custom-call | tf_op jit(solution)/shard_map/pallas_call | solution.py:231
  264.3 2.2 shard_map.262
  270.0 10.4 %collective-permute-done.40.refs_1_ = bf16[128,512]{1,0:T(8,128)(2,1)S(1)} collective-permute-done((bf16[128,512]{1,0:T(8,128)(2,1)}, bf16[128,512]{1,0:T(8,128)(2,1)S(1)}, u32[]{:S(2)}, u32[]{:S(2)}) %collective-permute-start.40) | collective-permute-done | bytes 131104 | tf_op jit(solution)/shard_map/ppermute | solution.py:64
  280.4 2.3 collective-permute-done.41.refs_2_
  283.4 1.9 shard_map.263
  291.0 7.3 %collective-permute-done.47.refs_8_ = bf16[128,512]{1,0:T(8,128)(2,1)S(1)} collective-permute-done((bf16[128,512]{1,0:T(8,128)(2,1)}, bf16[128,512]{1,0:T(8,128)(2,1)S(1)}, u32[]{:S(2)}, u32[]{:S(2)}) %collective-permute-start.47) | collective-permute-done | bytes 131104 | tf_op jit(solution)/shard_map/ppermute | solution.py:64
  301.5 6.3 %shard_map.265 = bf16[384,3584]{1,0:T(8,128)(2,1)} custom-call(bf16[512,384]{1,0:T(8,128)(2,1)} %bitcast.51, bf16[512,384]{1,0:T(8,128)(2,1)} %bitcast.7.refs_1_, bf16[128,3072]{1,0:T(8,128)(2,1)} %get-tuple-element.123.refs_0_.refs_2_, bf16[128,3072]{1,0:T(8,128)(2,1)} %copy-done.11, bf16[128,3072]{1,0:T(8,128)(2,1)} %copy-done.12, ...), custom_call_target="tpu_custom_call" | custom-call | tf_op jit(solution)/shard_map/pallas_call | solution.py:231
  309.4 2.2 collective-permute-done.50
  313.0 2.7 collective-permute-done.51
  321.2 2.5 collective-permute-done.53
  324.9 1.8 add_convert_fusion.4
  326.7 7.7 %shard_map.264 = f32[128,1536]{1,0:T(8,128)} custom-call(bf16[128,3072]{1,0:T(8,128)(2,1)} %get-tuple-element.123.refs_0_.refs_2_, bf16[128,512]{1,0:T(8,128)(2,1)} %get-tuple-element.121.refs_1_.refs_7_, bf16[128,1536]{1,0:T(8,128)(2,1)} %refs_2_.3, f32[128,1536]{1,0:T(8,128)} %get-tuple-element.124.refs_3_, f32[1,1536]{1,0:T(1,128)} %reshape.184.refs_1_.refs_4_, ...), custom_call_target="tpu_custom_call" | custom-call | tf_op jit(solution)/shard_map/pallas_call | solution.py:231
  335.7 9.1 %reduce-scatter.8.cloned.1.call-done = bf16[48,3584]{1,0:T(8,128)(2,1)} async-done(((bf16[384,3584]{1,0:T(8,128)(2,1)}), bf16[48,3584]{1,0:T(8,128)(2,1)}) %reduce-scatter.8.cloned.1.call-update) | async-done | bytes 344080 | tf_op jit(solution)/shard_map/reduce_scatter | solution.py:910
  347.2 9.3 %collective-permute-done.55.refs_1_ = bf16[2,280,1536]{2,1,0:T(8,128)(2,1)S(1)} collective-permute-done((bf16[2,280,1536]{2,1,0:T(8,128)(2,1)}, bf16[2,280,1536]{2,1,0:T(8,128)(2,1)S(1)}, u32[]{:S(2)}, u32[]{:S(2)}) %collective-permute-start.55) | collective-permute-done | bytes 1720352 | tf_op jit(solution)/shard_map/ppermute | solution.py:64
  358.1 5.7 %shard_map.266 = (f32[1536,280]{1,0:T(8,128)}, f32[1536,280]{1,0:T(8,128)}) custom-call(bf16[2,280,1536]{2,1,0:T(8,128)(2,1)} %get-tuple-element.101.refs_0_, bf16[2,280,1536]{2,1,0:T(8,128)(2,1)} %copy-done.13, bf16[2,280,1536]{2,1,0:T(8,128)(2,1)} %collective-permute-done.56.refs_2_), custom_call_target="tpu_custom_call" | custom-call | tf_op jit(solution)/shard_map/pallas_call | solution.py:668
  363.7 3.0 copy.58
  369.2 3.2 add_bitcast_fusion
  (304 shorter events, 98.6 us)
Async XLA Ops:
  7.2 37.7 %all-gather.6.cloned.1.call-start = ((), (), s32[]{:S(2)}) async-start(), calls=%async_computation.5 | async-start | bytes 1769472 | tf_op jit(solution)/shard_map/all_gather | solution.py:161
  10.4 102.2 %all-gather.12.cloned.1.call-start = ((), (), s32[]{:S(2)}) async-start(), calls=%async_computation.11 | async-start | bytes 5308416 | tf_op jit(solution)/shard_map/all_gather | solution.py:192
  14.3 8.7 %collective-permute-start.5 = (bf16[48,1536]{1,0:T(8,128)(2,1)}, bf16[48,1536]{1,0:T(8,128)(2,1)S(1)}, u32[]{:S(2)}, u32[]{:S(2)}) collective-permute-start(bf16[48,1536]{1,0:T(8,128)(2,1)} %param.24), channel_id=1, source_target_pairs={{0,8},{8,0},{16,24},{24,16},{1,9},{9,1},{17,25},{25,17},{2,10},{10... | collective-permute-start | bytes 442376 | tf_op jit(solution)/shard_map/ppermute | solution.py:64
  14.4 8.6 %collective-permute-start.6 = (bf16[48,1536]{1,0:T(8,128)(2,1)}, bf16[48,1536]{1,0:T(8,128)(2,1)S(1)}, u32[]{:S(2)}, u32[]{:S(2)}) collective-permute-start(bf16[48,1536]{1,0:T(8,128)(2,1)} %param.24), channel_id=1, source_target_pairs={{0,16},{8,24},{16,0},{24,8},{1,17},{9,25},{17,1},{25,9},{2,18},{10... | collective-permute-start | bytes 442376 | tf_op jit(solution)/shard_map/ppermute | solution.py:64
  24.0 19.9 %collective-permute-start.8 = (bf16[280,1536]{1,0:T(8,128)(2,1)}, bf16[280,1536]{1,0:T(8,128)(2,1)S(1)}, u32[]{:S(2)}, u32[]{:S(2)}) collective-permute-start(bf16[280,1536]{1,0:T(8,128)(2,1)} %param.28), channel_id=1, source_target_pairs={{0,8},{8,0},{16,24},{24,16},{1,9},{9,1},{17,25},{25,17},{2,10},{10... | collective-permute-start | bytes 2580488 | tf_op jit(solution)/shard_map/ppermute | solution.py:64
  25.6 19.4 %collective-permute-start.9 = (bf16[280,1536]{1,0:T(8,128)(2,1)}, bf16[280,1536]{1,0:T(8,128)(2,1)S(1)}, u32[]{:S(2)}, u32[]{:S(2)}) collective-permute-start(bf16[280,1536]{1,0:T(8,128)(2,1)} %param.28), channel_id=1, source_target_pairs={{0,16},{8,24},{16,0},{24,8},{1,17},{9,25},{17,1},{25,9},{2,18},{10... | collective-permute-start | bytes 2580488 | tf_op jit(solution)/shard_map/ppermute | solution.py:64
  45.0 115.7 %all-gather.10.cloned.1.call-start = ((), (), s32[]{:S(2)}) async-start(), calls=%async_computation.7 | async-start | bytes 3538944 | tf_op jit(solution)/shard_map/all_gather | solution.py:766
  50.4 22.4 %collective-permute-start.10 = (bf16[384,1024]{1,0:T(8,128)(2,1)}, bf16[384,1024]{1,0:T(8,128)(2,1)S(1)}, u32[]{:S(2)}, u32[]{:S(2)}) collective-permute-start(bf16[384,1024]{1,0:T(8,128)(2,1)} %constant_dynamic-slice_fusion.4), channel_id=1, source_target_pairs={{0,8},{8,0},{16,24},{24,16},{1,9},{9,1},{17,25},{25,17},{2,10},{10... | collective-permute-start | bytes 2359304 | tf_op jit(solution)/shard_map/ppermute | solution.py:64
  51.2 23.6 %collective-permute-start.11 = (bf16[384,1024]{1,0:T(8,128)(2,1)}, bf16[384,1024]{1,0:T(8,128)(2,1)S(1)}, u32[]{:S(2)}, u32[]{:S(2)}) collective-permute-start(bf16[384,1024]{1,0:T(8,128)(2,1)} %constant_dynamic-slice_fusion.4), channel_id=1, source_target_pairs={{0,16},{8,24},{16,0},{24,8},{1,17},{9,25},{17,1},{25,9},{2,18},{10... | collective-permute-start | bytes 2359304 | tf_op jit(solution)/shard_map/ppermute | solution.py:64
  56.5 16.3 %all-to-all-start = ((bf16[128,4,384]{2,0,1:T(8,128)(2,1)}), bf16[128,4,384]{2,0,1:T(8,128)(2,1)}, u32[]{:S(2)}, u32[]{:S(2)}) async-start(bf16[128,4,384]{2,0,1:T(8,128)(2,1)} %bitcast.53), calls=%async_computation | async-start | bytes 786432 | tf_op jit(solution)/shard_map/all_to_all | solution.py:732
  60.6 114.2 %all-gather.8.cloned.1.call-start = ((), (), s32[]{:S(2)}) async-start(), calls=%async_computation.6 | async-start | bytes 3538944 | tf_op jit(solution)/shard_map/all_gather | solution.py:819
  72.8 7.9 %collective-permute-start.12 = (bf16[384,512]{1,0:T(8,128)(2,1)S(1)}, bf16[384,512]{1,0:T(8,128)(2,1)S(1)}, u32[]{:S(2)}, u32[]{:S(2)}) collective-permute-start(bf16[384,512]{1,0:T(8,128)(2,1)S(1)} %slice.73), channel_id=1, source_target_pairs={{0,16},{8,24},{16,0},{24,8},{1,17},{9,25},{17,1},{25,9},{2,18},{10... | collective-permute-start | bytes 1179656 | tf_op jit(solution)/shard_map/ppermute | solution.py:64
  74.9 7.8 %collective-permute-start.13 = (bf16[384,512]{1,0:T(8,128)(2,1)S(1)}, bf16[384,512]{1,0:T(8,128)(2,1)S(1)}, u32[]{:S(2)}, u32[]{:S(2)}) collective-permute-start(bf16[384,512]{1,0:T(8,128)(2,1)S(1)} %slice.74), channel_id=1, source_target_pairs={{0,8},{8,0},{16,24},{24,16},{1,9},{9,1},{17,25},{25,17},{2,10},{10... | collective-permute-start | bytes 1179656 | tf_op jit(solution)/shard_map/ppermute | solution.py:64
  92.7 8.2 %collective-permute-start.19 = (bf16[128,512]{1,0:T(8,128)(2,1)}, bf16[128,512]{1,0:T(8,128)(2,1)S(1)}, u32[]{:S(2)}, u32[]{:S(2)}) collective-permute-start(bf16[128,512]{1,0:T(8,128)(2,1)} %get-tuple-element.83.refs_3_.refs_8_), channel_id=1, source_target_pairs={{0,16},{8,24},{16,0},{24,8},{1,17},{9,25},{17,1},{25,9},{2,18},{10... | collective-permute-start | bytes 393224 | tf_op jit(solution)/shard_map/ppermute | solution.py:64
  93.1 7.8 %collective-permute-start.20 = (bf16[128,512]{1,0:T(8,128)(2,1)}, bf16[128,512]{1,0:T(8,128)(2,1)S(1)}, u32[]{:S(2)}, u32[]{:S(2)}) collective-permute-start(bf16[128,512]{1,0:T(8,128)(2,1)} %get-tuple-element.83.refs_3_.refs_8_), channel_id=1, source_target_pairs={{0,24},{8,16},{16,8},{24,0},{1,25},{9,17},{17,9},{25,1},{2,26},{10... | collective-permute-start | bytes 393224 | tf_op jit(solution)/shard_map/ppermute | solution.py:64
  101.0 20.2 %collective-permute-start.25 = (bf16[280,1536]{1,0:T(8,128)(2,1)}, bf16[280,1536]{1,0:T(8,128)(2,1)S(1)}, u32[]{:S(2)}, u32[]{:S(2)}) collective-permute-start(bf16[280,1536]{1,0:T(8,128)(2,1)} %bitcast.17.refs_2_), channel_id=1, source_target_pairs={{0,8},{8,0},{16,24},{24,16},{1,9},{9,1},{17,25},{25,17},{2,10},{10... | collective-permute-start | bytes 2580488 | tf_op jit(solution)/shard_map/ppermute | solution.py:64
  101.6 20.0 %collective-permute-start.26 = (bf16[280,1536]{1,0:T(8,128)(2,1)}, bf16[280,1536]{1,0:T(8,128)(2,1)}, u32[]{:S(2)}, u32[]{:S(2)}) collective-permute-start(bf16[280,1536]{1,0:T(8,128)(2,1)} %bitcast.17.refs_2_), channel_id=1, source_target_pairs={{0,16},{8,24},{16,0},{24,8},{1,17},{9,25},{17,1},{25,9},{2,18},{10... | collective-permute-start | bytes 2580488 | tf_op jit(solution)/shard_map/ppermute | solution.py:64
  121.7 12.9 %collective-permute-start.28 = (bf16[280,768]{1,0:T(8,128)(2,1)S(1)}, bf16[280,768]{1,0:T(8,128)(2,1)S(1)}, u32[]{:S(2)}, u32[]{:S(2)}) collective-permute-start(bf16[280,768]{1,0:T(8,128)(2,1)S(1)} %slice.76), channel_id=1, source_target_pairs={{0,8},{8,0},{16,24},{24,16},{1,9},{9,1},{17,25},{25,17},{2,10},{10... | collective-permute-start | bytes 1290248 | tf_op jit(solution)/shard_map/ppermute | solution.py:64
  123.3 12.9 %collective-permute-start.27 = (bf16[280,768]{1,0:T(8,128)(2,1)S(1)}, bf16[280,768]{1,0:T(8,128)(2,1)S(1)}, u32[]{:S(2)}, u32[]{:S(2)}) collective-permute-start(bf16[280,768]{1,0:T(8,128)(2,1)S(1)} %slice.75), channel_id=1, source_target_pairs={{0,16},{8,24},{16,0},{24,8},{1,17},{9,25},{17,1},{25,9},{2,18},{10... | collective-permute-start | bytes 1290248 | tf_op jit(solution)/shard_map/ppermute | solution.py:64
  123.8 29.2 %collective-permute-start.31 = (bf16[280,1536]{1,0:T(8,128)(2,1)S(1)}, bf16[280,1536]{1,0:T(8,128)(2,1)S(1)}, u32[]{:S(2)}, u32[]{:S(2)}) collective-permute-start(bf16[280,1536]{1,0:T(8,128)(2,1)S(1)} %bitcast.56), channel_id=1, source_target_pairs={{0,8},{8,0},{16,24},{24,16},{1,9},{9,1},{17,25},{25,17},{2,10},{10... | collective-permute-start | bytes 2580488 | tf_op jit(solution)/shard_map/ppermute | solution.py:64
  125.5 29.1 %collective-permute-start.32 = (bf16[280,1536]{1,0:T(8,128)(2,1)S(1)}, bf16[280,1536]{1,0:T(8,128)(2,1)S(1)}, u32[]{:S(2)}, u32[]{:S(2)}) collective-permute-start(bf16[280,1536]{1,0:T(8,128)(2,1)S(1)} %bitcast.57), channel_id=1, source_target_pairs={{0,16},{8,24},{16,0},{24,8},{1,17},{9,25},{17,1},{25,9},{2,18},{10... | collective-permute-start | bytes 2580488 | tf_op jit(solution)/shard_map/ppermute | solution.py:64
  136.4 38.5 %collective-permute-start.29 = (bf16[280,768]{1,0:T(8,128)(2,1)S(1)}, bf16[280,768]{1,0:T(8,128)(2,1)}, u32[]{:S(2)}, u32[]{:S(2)}) collective-permute-start(bf16[280,768]{1,0:T(8,128)(2,1)S(1)} %slice.93), channel_id=1, source_target_pairs={{0,16},{8,24},{16,0},{24,8},{1,17},{9,25},{17,1},{25,9},{2,18},{10... | collective-permute-start | bytes 1290248 | tf_op jit(solution)/shard_map/ppermute | solution.py:64
  138.1 36.7 %collective-permute-start.30 = (bf16[280,768]{1,0:T(8,128)(2,1)S(1)}, bf16[280,768]{1,0:T(8,128)(2,1)}, u32[]{:S(2)}, u32[]{:S(2)}) collective-permute-start(bf16[280,768]{1,0:T(8,128)(2,1)S(1)} %slice.94), channel_id=1, source_target_pairs={{0,8},{8,0},{16,24},{24,16},{1,9},{9,1},{17,25},{25,17},{2,10},{10... | collective-permute-start | bytes 1290248 | tf_op jit(solution)/shard_map/ppermute | solution.py:64
  153.1 21.8 %collective-permute-start.33 = (bf16[280,768]{1,0:T(8,128)(2,1)S(1)}, bf16[280,768]{1,0:T(8,128)(2,1)}, u32[]{:S(2)}, u32[]{:S(2)}) collective-permute-start(bf16[280,768]{1,0:T(8,128)(2,1)S(1)} %slice.95), channel_id=1, source_target_pairs={{0,16},{8,24},{16,0},{24,8},{1,17},{9,25},{17,1},{25,9},{2,18},{10... | collective-permute-start | bytes 1290248 | tf_op jit(solution)/shard_map/ppermute | solution.py:64
  155.6 19.2 %collective-permute-start.34 = (bf16[280,768]{1,0:T(8,128)(2,1)S(1)}, bf16[280,768]{1,0:T(8,128)(2,1)}, u32[]{:S(2)}, u32[]{:S(2)}) collective-permute-start(bf16[280,768]{1,0:T(8,128)(2,1)S(1)} %slice.96), channel_id=1, source_target_pairs={{0,8},{8,0},{16,24},{24,16},{1,9},{9,1},{17,25},{25,17},{2,10},{10... | collective-permute-start | bytes 1290248 | tf_op jit(solution)/shard_map/ppermute | solution.py:64
  157.0 16.8 %all-to-all-start.1 = ((bf16[128,4,384]{2,0,1:T(8,128)(2,1)}), bf16[128,4,384]{2,0,1:T(8,128)(2,1)S(1)}, u32[]{:S(2)}, u32[]{:S(2)}) async-start(bf16[128,4,384]{2,0,1:T(8,128)(2,1)} %bitcast.46), calls=%async_computation.1 | async-start | bytes 786432 | tf_op jit(solution)/shard_map/all_to_all | solution.py:732
  160.4 82.6 %reduce-scatter.6.cloned.1.call-start = ((), (), s32[]{:S(2)}) async-start(), calls=%async_computation.9 | async-start | bytes 3538944 | tf_op jit(solution)/shard_map/reduce_scatter | solution.py:844
  198.3 121.8 %reduce-scatter.4.cloned.1.call-start = ((), (), s32[]{:S(2)}) async-start(), calls=%async_computation.8 | async-start | bytes 3538944 | tf_op jit(solution)/shard_map/reduce_scatter | solution.py:857
  214.0 130.8 %reduce-scatter.8.cloned.1.call-start = ((), (), s32[]{:S(2)}) async-start(), calls=%async_computation.10 | async-start | bytes 3096576 | tf_op jit(solution)/shard_map/reduce_scatter | solution.py:910
  214.9 16.8 %collective-permute-start.35 = (bf16[1,280,768]{2,1,0:T(8,128)(2,1)S(1)}, bf16[1,280,768]{2,1,0:T(8,128)(2,1)S(1)}, u32[]{:S(2)}, u32[]{:S(2)}) collective-permute-start(bf16[1,280,768]{2,1,0:T(8,128)(2,1)S(1)} %copy-done.53), channel_id=1, source_target_pairs={{0,16},{8,24},{16,0},{24,8},{1,17},{9,25},{17,1},{25,9},{2,18},{10... | collective-permute-start | bytes 1290248 | tf_op jit(solution)/shard_map/ppermute | solution.py:64
  229.1 12.8 %collective-permute-start.36 = (bf16[1,280,768]{2,1,0:T(8,128)(2,1)S(1)}, bf16[1,280,768]{2,1,0:T(8,128)(2,1)S(1)}, u32[]{:S(2)}, u32[]{:S(2)}) collective-permute-start(bf16[1,280,768]{2,1,0:T(8,128)(2,1)S(1)} %copy-done.52), channel_id=1, source_target_pairs={{0,8},{8,0},{16,24},{24,16},{1,9},{9,1},{17,25},{25,17},{2,10},{10... | collective-permute-start | bytes 1290248 | tf_op jit(solution)/shard_map/ppermute | solution.py:64
  230.6 29.5 %collective-permute-start.37 = (bf16[2,280,768]{2,1,0:T(8,128)(2,1)}, bf16[2,280,768]{2,1,0:T(8,128)(2,1)S(1)}, u32[]{:S(2)}, u32[]{:S(2)}) collective-permute-start(bf16[2,280,768]{2,1,0:T(8,128)(2,1)} %get-tuple-element.112), channel_id=1, source_target_pairs={{0,16},{8,24},{16,0},{24,8},{1,17},{9,25},{17,1},{25,9},{2,18},{10... | collective-permute-start | bytes 2580488 | tf_op jit(solution)/shard_map/ppermute | solution.py:64
  231.1 30.4 %collective-permute-start.38 = (bf16[2,280,768]{2,1,0:T(8,128)(2,1)}, bf16[2,280,768]{2,1,0:T(8,128)(2,1)S(1)}, u32[]{:S(2)}, u32[]{:S(2)}) collective-permute-start(bf16[2,280,768]{2,1,0:T(8,128)(2,1)} %get-tuple-element.114), channel_id=1, source_target_pairs={{0,8},{8,0},{16,24},{24,16},{1,9},{9,1},{17,25},{25,17},{2,10},{10... | collective-permute-start | bytes 2580488 | tf_op jit(solution)/shard_map/ppermute | solution.py:64
  258.3 27.0 %collective-permute-start.43 = (bf16[128,3072]{1,0:T(8,128)(2,1)}, bf16[128,3072]{1,0:T(8,128)(2,1)S(1)}, u32[]{:S(2)}, u32[]{:S(2)}) collective-permute-start(bf16[128,3072]{1,0:T(8,128)(2,1)} %get-tuple-element.123.refs_0_.refs_2_), channel_id=1, source_target_pairs={{0,8},{8,0},{16,24},{24,16},{1,9},{9,1},{17,25},{25,17},{2,10},{10... | collective-permute-start | bytes 2359304 | tf_op jit(solution)/shard_map/ppermute | solution.py:64
  259.9 26.1 %collective-permute-start.44 = (bf16[128,3072]{1,0:T(8,128)(2,1)}, bf16[128,3072]{1,0:T(8,128)(2,1)S(1)}, u32[]{:S(2)}, u32[]{:S(2)}) collective-permute-start(bf16[128,3072]{1,0:T(8,128)(2,1)} %get-tuple-element.123.refs_0_.refs_2_), channel_id=1, source_target_pairs={{0,16},{8,24},{16,0},{24,8},{1,17},{9,25},{17,1},{25,9},{2,18},{10... | collective-permute-start | bytes 2359304 | tf_op jit(solution)/shard_map/ppermute | solution.py:64
  266.5 13.9 %collective-permute-start.40 = (bf16[128,512]{1,0:T(8,128)(2,1)}, bf16[128,512]{1,0:T(8,128)(2,1)S(1)}, u32[]{:S(2)}, u32[]{:S(2)}) collective-permute-start(bf16[128,512]{1,0:T(8,128)(2,1)} %get-tuple-element.118), channel_id=1, source_target_pairs={{0,8},{8,0},{16,24},{24,16},{1,9},{9,1},{17,25},{25,17},{2,10},{10... | collective-permute-start | bytes 393224 | tf_op jit(solution)/shard_map/ppermute | solution.py:64
  267.1 15.6 %collective-permute-start.41 = (bf16[128,512]{1,0:T(8,128)(2,1)}, bf16[128,512]{1,0:T(8,128)(2,1)S(1)}, u32[]{:S(2)}, u32[]{:S(2)}) collective-permute-start(bf16[128,512]{1,0:T(8,128)(2,1)} %get-tuple-element.119), channel_id=1, source_target_pairs={{0,16},{8,24},{16,0},{24,8},{1,17},{9,25},{17,1},{25,9},{2,18},{10... | collective-permute-start | bytes 393224 | tf_op jit(solution)/shard_map/ppermute | solution.py:64
  268.9 13.8 %collective-permute-start.42 = (bf16[128,512]{1,0:T(8,128)(2,1)}, bf16[128,512]{1,0:T(8,128)(2,1)S(1)}, u32[]{:S(2)}, u32[]{:S(2)}) collective-permute-start(bf16[128,512]{1,0:T(8,128)(2,1)} %get-tuple-element.120), channel_id=1, source_target_pairs={{0,24},{8,16},{16,8},{24,0},{1,25},{9,17},{17,9},{25,1},{2,26},{10... | collective-permute-start | bytes 393224 | tf_op jit(solution)/shard_map/ppermute | solution.py:64
  285.3 14.6 %collective-permute-start.45 = (bf16[128,1536]{1,0:T(8,128)(2,1)S(1)}, bf16[128,1536]{1,0:T(8,128)(2,1)S(1)}, u32[]{:S(2)}, u32[]{:S(2)}) collective-permute-start(bf16[128,1536]{1,0:T(8,128)(2,1)S(1)} %slice.81), channel_id=1, source_target_pairs={{0,16},{8,24},{16,0},{24,8},{1,17},{9,25},{17,1},{25,9},{2,18},{10... | collective-permute-start | bytes 1179656 | tf_op jit(solution)/shard_map/ppermute | solution.py:64
  286.0 14.0 %collective-permute-start.46 = (bf16[128,1536]{1,0:T(8,128)(2,1)S(1)}, bf16[128,1536]{1,0:T(8,128)(2,1)S(1)}, u32[]{:S(2)}, u32[]{:S(2)}) collective-permute-start(bf16[128,1536]{1,0:T(8,128)(2,1)S(1)} %slice.82), channel_id=1, source_target_pairs={{0,8},{8,0},{16,24},{24,16},{1,9},{9,1},{17,25},{25,17},{2,10},{10... | collective-permute-start | bytes 1179656 | tf_op jit(solution)/shard_map/ppermute | solution.py:64
  287.5 10.8 %collective-permute-start.47 = (bf16[128,512]{1,0:T(8,128)(2,1)}, bf16[128,512]{1,0:T(8,128)(2,1)S(1)}, u32[]{:S(2)}, u32[]{:S(2)}) collective-permute-start(bf16[128,512]{1,0:T(8,128)(2,1)} %get-tuple-element.121.refs_1_.refs_7_), channel_id=1, source_target_pairs={{0,8},{8,0},{16,24},{24,16},{1,9},{9,1},{17,25},{25,17},{2,10},{10... | collective-permute-start | bytes 393224 | tf_op jit(solution)/shard_map/ppermute | solution.py:64
  288.1 10.2 %collective-permute-start.48 = (bf16[128,512]{1,0:T(8,128)(2,1)}, bf16[128,512]{1,0:T(8,128)(2,1)S(1)}, u32[]{:S(2)}, u32[]{:S(2)}) collective-permute-start(bf16[128,512]{1,0:T(8,128)(2,1)} %get-tuple-element.121.refs_1_.refs_7_), channel_id=1, source_target_pairs={{0,16},{8,24},{16,0},{24,8},{1,17},{9,25},{17,1},{25,9},{2,18},{10... | collective-permute-start | bytes 393224 | tf_op jit(solution)/shard_map/ppermute | solution.py:64
  289.6 10.4 %collective-permute-start.49 = (bf16[128,512]{1,0:T(8,128)(2,1)}, bf16[128,512]{1,0:T(8,128)(2,1)S(1)}, u32[]{:S(2)}, u32[]{:S(2)}) collective-permute-start(bf16[128,512]{1,0:T(8,128)(2,1)} %get-tuple-element.121.refs_1_.refs_7_), channel_id=1, source_target_pairs={{0,24},{8,16},{16,8},{24,0},{1,25},{9,17},{17,9},{25,1},{2,26},{10... | collective-permute-start | bytes 393224 | tf_op jit(solution)/shard_map/ppermute | solution.py:64
  315.7 40.8 %collective-permute-start.55 = (bf16[2,280,1536]{2,1,0:T(8,128)(2,1)}, bf16[2,280,1536]{2,1,0:T(8,128)(2,1)S(1)}, u32[]{:S(2)}, u32[]{:S(2)}) collective-permute-start(bf16[2,280,1536]{2,1,0:T(8,128)(2,1)} %add_convert_fusion.1), channel_id=1, source_target_pairs={{0,8},{8,0},{16,24},{24,16},{1,9},{9,1},{17,25},{25,17},{2,10},{10... | collective-permute-start | bytes 5160968 | tf_op jit(solution)/shard_map/ppermute | solution.py:64
  317.3 40.8 %collective-permute-start.56 = (bf16[2,280,1536]{2,1,0:T(8,128)(2,1)}, bf16[2,280,1536]{2,1,0:T(8,128)(2,1)}, u32[]{:S(2)}, u32[]{:S(2)}) collective-permute-start(bf16[2,280,1536]{2,1,0:T(8,128)(2,1)} %add_convert_fusion), channel_id=1, source_target_pairs={{0,16},{8,24},{16,0},{24,8},{1,17},{9,25},{17,1},{25,9},{2,18},{10... | collective-permute-start | bytes 5160968 | tf_op jit(solution)/shard_map/ppermute | solution.py:64
  320.1 49.0 %collective-permute-start.57 = (bf16[1,280,1536]{2,1,0:T(8,128)(2,1)}, bf16[1,280,1536]{2,1,0:T(8,128)(2,1)}, u32[]{:S(2)}, u32[]{:S(2)}) collective-permute-start(bf16[1,280,1536]{2,1,0:T(8,128)(2,1)} %add_convert_fusion.3), channel_id=1, source_target_pairs={{0,8},{8,0},{16,24},{24,16},{1,9},{9,1},{17,25},{25,17},{2,10},{10... | collective-permute-start | bytes 2580488 | tf_op jit(solution)/shard_map/ppermute | solution.py:64
  320.8 48.3 %collective-permute-start.58 = (bf16[1,280,1536]{2,1,0:T(8,128)(2,1)}, bf16[1,280,1536]{2,1,0:T(8,128)(2,1)}, u32[]{:S(2)}, u32[]{:S(2)}) collective-permute-start(bf16[1,280,1536]{2,1,0:T(8,128)(2,1)} %add_convert_fusion.2), channel_id=1, source_target_pairs={{0,16},{8,24},{16,0},{24,8},{1,17},{9,25},{17,1},{25,9},{2,18},{10... | collective-permute-start | bytes 2580488 | tf_op jit(solution)/shard_map/ppermute | solution.py:64
  323.8 10.7 %collective-permute-start.54 = (f32[1,3584]{1,0:T(1,128)S(1)}, f32[1,3584]{1,0:T(1,128)S(1)}, u32[]{:S(2)}, u32[]{:S(2)}) collective-permute-start(f32[1,3584]{1,0:T(1,128)S(1)} %add.134), channel_id=1, source_target_pairs={{0,2},{1,3},{2,0},{3,1},{4,6},{5,7},{6,4},{7,5},{8,10},{9,11},{10,... | collective-permute-start | bytes 43016 | tf_op jit(solution)/shard_map/ppermute | solution.py:699
  (74 other events, 604.0 us)
Sparse Core Ops, SparseCore 0:
  10.5 28.9 all-gather.5
  45.1 52.2 all-gather.11
  99.0 37.0 all-gather.9
  137.6 37.1 all-gather.7
  198.4 40.0 reduce-scatter.5
  240.7 39.4 reduce-scatter.3
  308.0 36.7 reduce-scatter.7

commit v2 on v1

--- a/solution.py
+++ b/solution.py
@@ -772,7 +772,7 @@
     matches = from_ctx[:, None] == steps[None, :]
     key_places = jnp.sum(jnp.where(matches[:, :, None], places[None], 0), axis=1)
     key_places = key_places.reshape(-1, 2, rows // 2).transpose(1, 0, 2).reshape(1, -1)
-    unit_columns = columns(after(unit, qkv_near[0]))
+    unit_columns = columns(unit)
     ready = (unit_columns, gain_one, gain_two, bias_qkv, cosine, sine, key_places)
     weight_qkv = gather_weight(qkv_rows, qkv_near, ready)
     if output_weight.shape[0] % 16:

time: 381 us -> 382 us (level)
    ppermute x40, waiting for transfers between devices: 86 us -> 97.8 us  [exchange(): return lax.ppermute(values, 'grp', [(i, i ^ bit) for i in range(count)])]
    all_to_all x2, waiting for transfers between devices: 14.9 us -> 3.75 us  [columns(): lax.all_to_all(values, 'grp', split_axis=1, concat_axis=0, tiled=True)]
    unnamed x120 -> x130, local copies, waits for them, and re-layouts: 13.7 us -> 14.5 us
  transfers between devices with their start and end apart: 68 -> 68, of which waited for: 35 -> 36; matrix products, arithmetic and copies ran while one was open for 13% -> 12% of each run, Pallas kernels for 20% -> 20%
where the time goes in v2:
time: 382 us; the launch traced here: 381 us
  waiting for transfers between devices  138 us (36%)
  Pallas kernels  100 us (26%)
  starting transfers between devices  68.4 us (18%)
  local copies, waits for them, and re-layouts  26.7 us (7%)
  other arithmetic  16.6 us (4%)
  matrix products  16.3 us (4%)
  between operations  14.9 us (4%)
    ppermute x40, waiting for transfers between devices, exchange(): return lax.ppermute(values, 'grp', [(i, i ^ bit) for i in range(count)])  97.8 us
    pallas_call x9, Pallas kernels, call(): pl.pallas_call(kernel, out_shape=[jax.ShapeDtypeStruct(shape, dtype) for...  50.7 us
    ppermute x40, starting transfers between devices, exchange(): return lax.ppermute(values, 'grp', [(i, i ^ bit) for i in range(count)])  47.3 us
    pallas_call x1, Pallas kernels, forward_back(): pl.pallas_call(lambda *refs: forward_back_kernel(count, refs), grid=(toke...  23.4 us
    pallas_call x2, Pallas kernels, outer(): pl.pallas_call(lambda *refs: outer_kernel(refs), grid=(stack, 2), out_sha...  20.7 us
    ppermute x10, waiting for transfers between devices, sum_over(): lax.ppermute(values, axis, [(i, i ^ bit) for i in range(count)])  20.5 us
    unnamed x130, local copies, waits for them, and re-layouts  14.5 us
    ppermute x10, starting transfers between devices, sum_over(): lax.ppermute(values, axis, [(i, i ^ bit) for i in range(count)])  12.5 us
  transfers between devices with their start and end apart: 68, of which 36 were waited for; matrix products, arithmetic and copies ran while one was open for 12% of the time, Pallas kernels for 20%

profile of v2, /device:TPU:0, one launch (start us, length us, event | category | flops | bytes accessed | tf_op | source)
XLA Modules:
  0.0 381.1 jit_solution(14996150067260971711)
XLA Ops:
  11.3 3.0 collective-permute-start
  14.4 2.0 collective-permute-start.6
  19.5 3.5 collective-permute-done.1
  29.9 4.2 %collective-permute-done.3 = f32[32,160]{1,0:T(8,128)S(1)} collective-permute-done((f32[32,160]{1,0:T(8,128)S(1)}, f32[32,160]{1,0:T(8,128)S(1)}, u32[]{:S(2)}, u32[]{:S(2)}) %collective-permute-start.3) | collective-permute-done | bytes 20512 | tf_op jit(solution)/shard_map/ppermute | solution.py:699
  35.5 3.4 collective-permute-done.4
  39.0 1.8 pad_maximum_fusion
  40.8 3.2 collective-permute-done.8
  46.8 3.6 all-to-all-start
  53.0 2.0 collective-permute-start.10
  60.3 12.1 %collective-permute-done.10.refs_6_ = bf16[384,1024]{1,0:T(8,128)(2,1)S(1)} collective-permute-done((bf16[384,1024]{1,0:T(8,128)(2,1)}, bf16[384,1024]{1,0:T(8,128)(2,1)S(1)}, u32[]{:S(2)}, u32[]{:S(2)}) %collective-permute-start.10) | collective-permute-done | bytes 786464 | tf_op jit(solution)/shard_map/ppermute | solution.py:64
  75.9 5.7 %collective-permute-done.12.refs_8_ = bf16[384,512]{1,0:T(8,128)(2,1)S(1)} collective-permute-done((bf16[384,512]{1,0:T(8,128)(2,1)S(1)}, bf16[384,512]{1,0:T(8,128)(2,1)S(1)}, u32[]{:S(2)}, u32[]{:S(2)}) %collective-permute-start.12) | collective-permute-done | bytes 393248 | tf_op jit(solution)/shard_map/ppermute | solution.py:64
  85.1 5.7 %shard_map.254 = (bf16[128,1536]{1,0:T(8,128)(2,1)}, bf16[1536,128]{1,0:T(8,128)(2,1)}, bf16[128,512]{1,0:T(8,128)(2,1)}) custom-call(bf16[128,1536]{1,0:T(8,128)(2,1)} %refs_2_.3, f32[1,1536]{1,0:T(1,128)} %reshape.184.refs_1_.refs_4_, f32[1,2048]{1,0:T(1,128)} %bitcast.62, f32[128,128]{1,0:T(8,128)} %pad_maximum_fusion.1.refs_3_.refs_5_.refs_4_, ...), custom_call_target="tpu_custom_call" | custom-call | tf_op jit(solution)/shard_map/pallas_call | solution.py:231
  94.4 2.4 collective-permute-done.18.refs_4_.refs_9_
  96.9 4.1 %collective-permute-done.19.refs_5_.refs_10_ = bf16[128,512]{1,0:T(8,128)(2,1)S(1)} collective-permute-done((bf16[128,512]{1,0:T(8,128)(2,1)}, bf16[128,512]{1,0:T(8,128)(2,1)S(1)}, u32[]{:S(2)}, u32[]{:S(2)}) %collective-permute-start.19) | collective-permute-done | bytes 131104 | tf_op jit(solution)/shard_map/ppermute | solution.py:64
  106.4 6.2 %shard_map.255 = (bf16[128,1536]{1,0:T(8,128)(2,1)}, f32[1536,1]{1,0:T(8,128)}) custom-call(bf16[1536,128]{1,0:T(8,128)(2,1)} %get-tuple-element.80.refs_0_, s32[1,1024]{1,0:T(1,128)} %reshape.191.refs_1_.refs_3_, s32[128,1]{1,0:T(8,128)} %copy.54.refs_2_.refs_4_, bf16[128,512]{1,0:T(8,128)(2,1)} %get-tuple-element.81.refs_3_.refs_8_, ...), custom_call_target="tpu_custom_call" | custom-call | tf_op jit(solution)/shard_map/pallas_call | solution.py:231
  112.6 5.5 %shard_map.256 = (f32[128,1536]{1,0:T(8,128)}, bf16[128,1536]{1,0:T(8,128)(2,1)}) custom-call(bf16[128,1536]{1,0:T(8,128)(2,1)} %get-tuple-element.88.refs_0_, bf16[128,1536]{1,0:T(8,128)(2,1)} %refs_2_.3, f32[1,1536]{1,0:T(1,128)} %reshape.189.refs_2_.refs_3_, bf16[8,4,48,1536]{3,2,1,0:T(8,128)(2,1)} %bitcast.48), custom_call_target="tpu_custom_call" | custom-call | tf_op jit(solution)/shard_map/pallas_call | solution.py:231
  118.1 2.3 collective-permute-done.25.refs_3_
  123.7 1.8 collective-permute-start.31
  126.5 8.5 %collective-permute-done.28 = bf16[280,768]{1,0:T(8,128)(2,1)S(1)} collective-permute-done((bf16[280,768]{1,0:T(8,128)(2,1)S(1)}, bf16[280,768]{1,0:T(8,128)(2,1)S(1)}, u32[]{:S(2)}, u32[]{:S(2)}) %collective-permute-start.28) | collective-permute-done | bytes 430112 | tf_op jit(solution)/shard_map/ppermute | solution.py:64
  137.7 1.8 collective-permute-start.30
  139.5 13.9 %collective-permute-done.31.refs_8_ = bf16[280,1536]{1,0:T(8,128)(2,1)S(1)} collective-permute-done((bf16[280,1536]{1,0:T(8,128)(2,1)S(1)}, bf16[280,1536]{1,0:T(8,128)(2,1)S(1)}, u32[]{:S(2)}, u32[]{:S(2)}) %collective-permute-start.31) | collective-permute-done | bytes 860192 | tf_op jit(solution)/shard_map/ppermute | solution.py:64
  157.4 3.5 all-to-all-start.1
  161.1 8.7 %fusion.refs_1_ = bf16[1024,1152]{1,0:T(8,128)(2,1)} fusion(bf16[1152,1536]{1,0:T(8,128)(2,1)} %copy-done.44, bf16[1024,1536]{1,0:T(8,128)(2,1)} %all-gather.10.cloned.1.call-done.refs_1_), kind=kOutput, calls=%fused_computation.3 | convolution fusion | flops 3625058304 | bytes 9043968 | tf_op jit(solution)/shard_map/dot_general | solution.py:43
  169.8 3.7 all-to-all-done.1
  173.5 1.9 all-gather.8.cloned.1.call-done.refs_0_.refs_1_
  176.2 23.4 %shard_map.257 = (bf16[1,1024,1152]{2,1,0:T(8,128)(2,1)}, bf16[2,1024,1152]{2,1,0:T(8,128)(2,1)}, bf16[1024,1536]{1,0:T(8,128)(2,1)}) custom-call(bf16[1024,1536]{1,0:T(8,128)(2,1)} %all-gather.8.cloned.1.call-done.refs_0_.refs_1_, bf16[1024,1152]{1,0:T(8,128)(2,1)} %fusion.refs_1_, bf16[280,1536]{1,0:T(8,128)(2,1)} %bitcast.17.refs_2_, ...), custom_call_target="tpu_custom_call" | custom-call | tf_op jit(solution)/shard_map/pallas_call | solution.py:582
  199.7 8.1 %shard_map.258 = (bf16[1,280,1536]{2,1,0:T(8,128)(2,1)}, bf16[1,280,1536]{2,1,0:T(8,128)(2,1)}, bf16[1,280,1536]{2,1,0:T(8,128)(2,1)}, bf16[1,280,768]{2,1,0:T(8,128)(2,1)}, bf16[1,280,768]{2,1,0:T(8,128)(2,1)}) custom-call(bf16[1,1024,1152]{2,1,0:T(8,128)(2,1)} %get-tuple-element.93.refs_0_, bf16[1024,1536]{1,0:T(8,128)(2,1)} %all-gather.10.cloned.1.call-done.refs_1_), custom_call_target="tpu_custom_call" | custom-call | tf_op jit(solution)/shard_map/pallas_call | solution.py:629
  207.8 7.6 %fusion.13 = bf16[1024,1536]{1,0:T(8,128)(2,1)} fusion(bf16[1024,1152]{1,0:T(8,128)(2,1)S(1)} %bitcast.50, bf16[1152,1536]{1,0:T(8,128)(2,1)} %copy-done.44), kind=kOutput, calls=%fused_computation.59 | convolution fusion | flops 3623878656 | bytes 9043968 | tf_op jit(solution)/shard_map/dot_general | solution.py:39
  217.9 12.6 %shard_map.259 = (bf16[2,280,1536]{2,1,0:T(8,128)(2,1)}, bf16[2,280,1536]{2,1,0:T(8,128)(2,1)}, bf16[2,280,1536]{2,1,0:T(8,128)(2,1)}, bf16[2,280,768]{2,1,0:T(8,128)(2,1)}, bf16[2,280,768]{2,1,0:T(8,128)(2,1)}) custom-call(bf16[2,1024,1152]{2,1,0:T(8,128)(2,1)} %get-tuple-element.98.refs_0_, bf16[1024,1536]{1,0:T(8,128)(2,1)} %all-gather.8.cloned.1.call-done.refs_0_.refs_1_), custom_call_target="tpu_custom_call" | custom-call | tf_op jit(solution)/shard_map/pallas_call | solution.py:629
  234.2 9.1 %collective-permute-done.36 = bf16[1,280,768]{2,1,0:T(8,128)(2,1)S(1)} collective-permute-done((bf16[1,280,768]{2,1,0:T(8,128)(2,1)S(1)}, bf16[1,280,768]{2,1,0:T(8,128)(2,1)S(1)}, u32[]{:S(2)}, u32[]{:S(2)}) %collective-permute-start.36) | collective-permute-done | bytes 430112 | tf_op jit(solution)/shard_map/ppermute | solution.py:64
  244.4 6.3 %shard_map.260 = (f32[128,1536]{1,0:T(8,128)}, bf16[128,1536]{1,0:T(8,128)(2,1)}, bf16[1536,128]{1,0:T(8,128)(2,1)}, f32[1,1536]{1,0:T(1,128)}) custom-call(bf16[128,1536]{1,0:T(8,128)(2,1)} %reduce-scatter.6.cloned.1.call-done.refs_0_, f32[128,1536]{1,0:T(8,128)} %get-tuple-element.84.refs_1_, bf16[128,1536]{1,0:T(8,128)(2,1)} %refs_2_.2, ...), custom_call_target="tpu_custom_call" | custom-call | tf_op jit(solution)/shard_map/pallas_call | solution.py:231
  250.7 8.9 %shard_map.261 = (bf16[128,3072]{1,0:T(8,128)(2,1)}, f32[1,1536]{1,0:T(1,128)}, f32[512,512]{1,0:T(8,128)}, bf16[512,512]{1,0:T(8,128)(2,1)}) custom-call(bf16[1536,128]{1,0:T(8,128)(2,1)} %get-tuple-element.80.refs_0_, bf16[1536,128]{1,0:T(8,128)(2,1)} %get-tuple-element.105.refs_1_, f32[1536,1]{1,0:T(8,128)} %get-tuple-element.106.refs_2_, ...), custom_call_target="tpu_custom_call" | custom-call | tf_op jit(solution)/shard_map/pallas_call | solution.py:231
  266.0 2.2 shard_map.262
  271.7 10.2 %collective-permute-done.40.refs_1_ = bf16[128,512]{1,0:T(8,128)(2,1)S(1)} collective-permute-done((bf16[128,512]{1,0:T(8,128)(2,1)}, bf16[128,512]{1,0:T(8,128)(2,1)S(1)}, u32[]{:S(2)}, u32[]{:S(2)}) %collective-permute-start.40) | collective-permute-done | bytes 131104 | tf_op jit(solution)/shard_map/ppermute | solution.py:64
  281.9 2.4 collective-permute-done.41.refs_2_
  285.0 1.9 shard_map.263
  292.6 7.1 %collective-permute-done.47.refs_8_ = bf16[128,512]{1,0:T(8,128)(2,1)S(1)} collective-permute-done((bf16[128,512]{1,0:T(8,128)(2,1)}, bf16[128,512]{1,0:T(8,128)(2,1)S(1)}, u32[]{:S(2)}, u32[]{:S(2)}) %collective-permute-start.47) | collective-permute-done | bytes 131104 | tf_op jit(solution)/shard_map/ppermute | solution.py:64
  302.5 6.3 %shard_map.265 = bf16[384,3584]{1,0:T(8,128)(2,1)} custom-call(bf16[512,384]{1,0:T(8,128)(2,1)} %bitcast.52, bf16[512,384]{1,0:T(8,128)(2,1)} %bitcast.51, bf16[128,3072]{1,0:T(8,128)(2,1)} %get-tuple-element.121.refs_0_.refs_2_, bf16[128,3072]{1,0:T(8,128)(2,1)} %copy-done.14, bf16[128,3072]{1,0:T(8,128)(2,1)} %copy-done.15, bf16[128,1536]{1,0:T(8,128)(2,1)} %copy-done.42, ...), custom_call_target="tpu_custom_call" | custom-call | tf_op jit(solution)/shard_map/pallas_call | solution.py:231
  310.5 2.3 collective-permute-done.50
  314.4 2.4 collective-permute-done.51
  322.9 2.3 collective-permute-done.53
  326.4 1.8 add_convert_fusion.4
  328.2 7.8 %shard_map.264 = f32[128,1536]{1,0:T(8,128)} custom-call(bf16[128,3072]{1,0:T(8,128)(2,1)} %get-tuple-element.121.refs_0_.refs_2_, bf16[128,512]{1,0:T(8,128)(2,1)} %get-tuple-element.119.refs_1_.refs_7_, bf16[128,1536]{1,0:T(8,128)(2,1)} %refs_2_.3, f32[128,1536]{1,0:T(8,128)} %get-tuple-element.122.refs_3_, f32[1,1536]{1,0:T(1,128)} %reshape.184.refs_1_.refs_4_, ...), custom_call_target="tpu_custom_call" | custom-call | tf_op jit(solution)/shard_map/pallas_call | solution.py:231
  337.1 9.0 %reduce-scatter.8.cloned.1.call-done = bf16[48,3584]{1,0:T(8,128)(2,1)} async-done(((bf16[384,3584]{1,0:T(8,128)(2,1)}), bf16[48,3584]{1,0:T(8,128)(2,1)}) %reduce-scatter.8.cloned.1.call-update) | async-done | bytes 344080 | tf_op jit(solution)/shard_map/reduce_scatter | solution.py:910
  348.6 9.0 %collective-permute-done.55.refs_1_ = bf16[2,280,1536]{2,1,0:T(8,128)(2,1)S(1)} collective-permute-done((bf16[2,280,1536]{2,1,0:T(8,128)(2,1)}, bf16[2,280,1536]{2,1,0:T(8,128)(2,1)S(1)}, u32[]{:S(2)}, u32[]{:S(2)}) %collective-permute-start.55) | collective-permute-done | bytes 1720352 | tf_op jit(solution)/shard_map/ppermute | solution.py:64
  359.2 5.7 %shard_map.266 = (f32[1536,280]{1,0:T(8,128)}, f32[1536,280]{1,0:T(8,128)}) custom-call(bf16[2,280,1536]{2,1,0:T(8,128)(2,1)} %get-tuple-element.99.refs_0_, bf16[2,280,1536]{2,1,0:T(8,128)(2,1)} %copy-done.16, bf16[2,280,1536]{2,1,0:T(8,128)(2,1)} %collective-permute-done.56.refs_2_), custom_call_target="tpu_custom_call" | custom-call | tf_op jit(solution)/shard_map/pallas_call | solution.py:668
  364.9 3.0 copy.58
  370.3 3.2 add_bitcast_fusion
  (314 shorter events, 99.2 us)
Async XLA Ops:
  7.2 37.7 %all-gather.6.cloned.1.call-start = ((), (), s32[]{:S(2)}) async-start(), calls=%async_computation.5 | async-start | bytes 1769472 | tf_op jit(solution)/shard_map/all_gather | solution.py:161
  10.4 102.2 %all-gather.12.cloned.1.call-start = ((), (), s32[]{:S(2)}) async-start(), calls=%async_computation.11 | async-start | bytes 5308416 | tf_op jit(solution)/shard_map/all_gather | solution.py:192
  14.3 8.7 %collective-permute-start.5 = (bf16[48,1536]{1,0:T(8,128)(2,1)}, bf16[48,1536]{1,0:T(8,128)(2,1)S(1)}, u32[]{:S(2)}, u32[]{:S(2)}) collective-permute-start(bf16[48,1536]{1,0:T(8,128)(2,1)} %param.24), channel_id=1, source_target_pairs={{0,8},{8,0},{16,24},{24,16},{1,9},{9,1},{17,25},{25,17},{2,10},{10... | collective-permute-start | bytes 442376 | tf_op jit(solution)/shard_map/ppermute | solution.py:64
  14.4 8.6 %collective-permute-start.6 = (bf16[48,1536]{1,0:T(8,128)(2,1)}, bf16[48,1536]{1,0:T(8,128)(2,1)S(1)}, u32[]{:S(2)}, u32[]{:S(2)}) collective-permute-start(bf16[48,1536]{1,0:T(8,128)(2,1)} %param.24), channel_id=1, source_target_pairs={{0,16},{8,24},{16,0},{24,8},{1,17},{9,25},{17,1},{25,9},{2,18},{10... | collective-permute-start | bytes 442376 | tf_op jit(solution)/shard_map/ppermute | solution.py:64
  16.4 7.6 %collective-permute-start.7 = (bf16[48,1536]{1,0:T(8,128)(2,1)}, bf16[48,1536]{1,0:T(8,128)(2,1)S(1)}, u32[]{:S(2)}, u32[]{:S(2)}) collective-permute-start(bf16[48,1536]{1,0:T(8,128)(2,1)} %param.24), channel_id=1, source_target_pairs={{0,24},{8,16},{16,8},{24,0},{1,25},{9,17},{17,9},{25,1},{2,26},{10... | collective-permute-start | bytes 442376 | tf_op jit(solution)/shard_map/ppermute | solution.py:64
  24.0 19.9 %collective-permute-start.8 = (bf16[280,1536]{1,0:T(8,128)(2,1)}, bf16[280,1536]{1,0:T(8,128)(2,1)S(1)}, u32[]{:S(2)}, u32[]{:S(2)}) collective-permute-start(bf16[280,1536]{1,0:T(8,128)(2,1)} %param.28), channel_id=1, source_target_pairs={{0,8},{8,0},{16,24},{24,16},{1,9},{9,1},{17,25},{25,17},{2,10},{10... | collective-permute-start | bytes 2580488 | tf_op jit(solution)/shard_map/ppermute | solution.py:64
  25.6 19.4 %collective-permute-start.9 = (bf16[280,1536]{1,0:T(8,128)(2,1)}, bf16[280,1536]{1,0:T(8,128)(2,1)S(1)}, u32[]{:S(2)}, u32[]{:S(2)}) collective-permute-start(bf16[280,1536]{1,0:T(8,128)(2,1)} %param.28), channel_id=1, source_target_pairs={{0,16},{8,24},{16,0},{24,8},{1,17},{9,25},{17,1},{25,9},{2,18},{10... | collective-permute-start | bytes 2580488 | tf_op jit(solution)/shard_map/ppermute | solution.py:64
  45.0 116.1 %all-gather.10.cloned.1.call-start = ((), (), s32[]{:S(2)}) async-start(), calls=%async_computation.7 | async-start | bytes 3538944 | tf_op jit(solution)/shard_map/all_gather | solution.py:766
  46.8 13.5 %all-to-all-start = ((bf16[128,4,384]{2,0,1:T(8,128)(2,1)}), bf16[128,4,384]{2,0,1:T(8,128)(2,1)S(1)}, u32[]{:S(2)}, u32[]{:S(2)}) async-start(bf16[128,4,384]{2,0,1:T(8,128)(2,1)} %bitcast.47), calls=%async_computation | async-start | bytes 786432 | tf_op jit(solution)/shard_map/all_to_all | solution.py:732
  50.4 125.0 %all-gather.8.cloned.1.call-start = ((), (), s32[]{:S(2)}) async-start(), calls=%async_computation.6 | async-start | bytes 3538944 | tf_op jit(solution)/shard_map/all_gather | solution.py:819
  53.0 19.4 %collective-permute-start.10 = (bf16[384,1024]{1,0:T(8,128)(2,1)}, bf16[384,1024]{1,0:T(8,128)(2,1)S(1)}, u32[]{:S(2)}, u32[]{:S(2)}) collective-permute-start(bf16[384,1024]{1,0:T(8,128)(2,1)} %constant_dynamic-slice_fusion.4), channel_id=1, source_target_pairs={{0,8},{8,0},{16,24},{24,16},{1,9},{9,1},{17,25},{25,17},{2,10},{10... | collective-permute-start | bytes 2359304 | tf_op jit(solution)/shard_map/ppermute | solution.py:64
  55.0 19.2 %collective-permute-start.11 = (bf16[384,1024]{1,0:T(8,128)(2,1)}, bf16[384,1024]{1,0:T(8,128)(2,1)S(1)}, u32[]{:S(2)}, u32[]{:S(2)}) collective-permute-start(bf16[384,1024]{1,0:T(8,128)(2,1)} %constant_dynamic-slice_fusion.4), channel_id=1, source_target_pairs={{0,16},{8,24},{16,0},{24,8},{1,17},{9,25},{17,1},{25,9},{2,18},{10... | collective-permute-start | bytes 2359304 | tf_op jit(solution)/shard_map/ppermute | solution.py:64
  72.4 9.1 %collective-permute-start.12 = (bf16[384,512]{1,0:T(8,128)(2,1)S(1)}, bf16[384,512]{1,0:T(8,128)(2,1)S(1)}, u32[]{:S(2)}, u32[]{:S(2)}) collective-permute-start(bf16[384,512]{1,0:T(8,128)(2,1)S(1)} %slice.73), channel_id=1, source_target_pairs={{0,16},{8,24},{16,0},{24,8},{1,17},{9,25},{17,1},{25,9},{2,18},{10... | collective-permute-start | bytes 1179656 | tf_op jit(solution)/shard_map/ppermute | solution.py:64
  74.2 8.4 %collective-permute-start.13 = (bf16[384,512]{1,0:T(8,128)(2,1)S(1)}, bf16[384,512]{1,0:T(8,128)(2,1)S(1)}, u32[]{:S(2)}, u32[]{:S(2)}) collective-permute-start(bf16[384,512]{1,0:T(8,128)(2,1)S(1)} %slice.74), channel_id=1, source_target_pairs={{0,8},{8,0},{16,24},{24,16},{1,9},{9,1},{17,25},{25,17},{2,10},{10... | collective-permute-start | bytes 1179656 | tf_op jit(solution)/shard_map/ppermute | solution.py:64
  92.7 8.3 %collective-permute-start.19 = (bf16[128,512]{1,0:T(8,128)(2,1)}, bf16[128,512]{1,0:T(8,128)(2,1)S(1)}, u32[]{:S(2)}, u32[]{:S(2)}) collective-permute-start(bf16[128,512]{1,0:T(8,128)(2,1)} %get-tuple-element.81.refs_3_.refs_8_), channel_id=1, source_target_pairs={{0,16},{8,24},{16,0},{24,8},{1,17},{9,25},{17,1},{25,9},{2,18},{10... | collective-permute-start | bytes 393224 | tf_op jit(solution)/shard_map/ppermute | solution.py:64
  101.0 19.4 %collective-permute-start.25 = (bf16[280,1536]{1,0:T(8,128)(2,1)}, bf16[280,1536]{1,0:T(8,128)(2,1)S(1)}, u32[]{:S(2)}, u32[]{:S(2)}) collective-permute-start(bf16[280,1536]{1,0:T(8,128)(2,1)} %bitcast.17.refs_2_), channel_id=1, source_target_pairs={{0,8},{8,0},{16,24},{24,16},{1,9},{9,1},{17,25},{25,17},{2,10},{10... | collective-permute-start | bytes 2580488 | tf_op jit(solution)/shard_map/ppermute | solution.py:64
  101.6 20.4 %collective-permute-start.26 = (bf16[280,1536]{1,0:T(8,128)(2,1)}, bf16[280,1536]{1,0:T(8,128)(2,1)}, u32[]{:S(2)}, u32[]{:S(2)}) collective-permute-start(bf16[280,1536]{1,0:T(8,128)(2,1)} %bitcast.17.refs_2_), channel_id=1, source_target_pairs={{0,16},{8,24},{16,0},{24,8},{1,17},{9,25},{17,1},{25,9},{2,18},{10... | collective-permute-start | bytes 2580488 | tf_op jit(solution)/shard_map/ppermute | solution.py:64
  122.1 12.9 %collective-permute-start.28 = (bf16[280,768]{1,0:T(8,128)(2,1)S(1)}, bf16[280,768]{1,0:T(8,128)(2,1)S(1)}, u32[]{:S(2)}, u32[]{:S(2)}) collective-permute-start(bf16[280,768]{1,0:T(8,128)(2,1)S(1)} %slice.76), channel_id=1, source_target_pairs={{0,8},{8,0},{16,24},{24,16},{1,9},{9,1},{17,25},{25,17},{2,10},{10... | collective-permute-start | bytes 1290248 | tf_op jit(solution)/shard_map/ppermute | solution.py:64
  122.5 12.9 %collective-permute-start.27 = (bf16[280,768]{1,0:T(8,128)(2,1)S(1)}, bf16[280,768]{1,0:T(8,128)(2,1)S(1)}, u32[]{:S(2)}, u32[]{:S(2)}) collective-permute-start(bf16[280,768]{1,0:T(8,128)(2,1)S(1)} %slice.75), channel_id=1, source_target_pairs={{0,16},{8,24},{16,0},{24,8},{1,17},{9,25},{17,1},{25,9},{2,18},{10... | collective-permute-start | bytes 1290248 | tf_op jit(solution)/shard_map/ppermute | solution.py:64
  123.7 29.7 %collective-permute-start.31 = (bf16[280,1536]{1,0:T(8,128)(2,1)S(1)}, bf16[280,1536]{1,0:T(8,128)(2,1)S(1)}, u32[]{:S(2)}, u32[]{:S(2)}) collective-permute-start(bf16[280,1536]{1,0:T(8,128)(2,1)S(1)} %bitcast.56), channel_id=1, source_target_pairs={{0,8},{8,0},{16,24},{24,16},{1,9},{9,1},{17,25},{25,17},{2,10},{10... | collective-permute-start | bytes 2580488 | tf_op jit(solution)/shard_map/ppermute | solution.py:64
  125.6 29.1 %collective-permute-start.32 = (bf16[280,1536]{1,0:T(8,128)(2,1)S(1)}, bf16[280,1536]{1,0:T(8,128)(2,1)S(1)}, u32[]{:S(2)}, u32[]{:S(2)}) collective-permute-start(bf16[280,1536]{1,0:T(8,128)(2,1)S(1)} %bitcast.57), channel_id=1, source_target_pairs={{0,16},{8,24},{16,0},{24,8},{1,17},{9,25},{17,1},{25,9},{2,18},{10... | collective-permute-start | bytes 2580488 | tf_op jit(solution)/shard_map/ppermute | solution.py:64
  135.5 39.9 %collective-permute-start.29 = (bf16[280,768]{1,0:T(8,128)(2,1)S(1)}, bf16[280,768]{1,0:T(8,128)(2,1)S(1)}, u32[]{:S(2)}, u32[]{:S(2)}) collective-permute-start(bf16[280,768]{1,0:T(8,128)(2,1)S(1)} %slice.93), channel_id=1, source_target_pairs={{0,16},{8,24},{16,0},{24,8},{1,17},{9,25},{17,1},{25,9},{2,18},{10... | collective-permute-start | bytes 1290248 | tf_op jit(solution)/shard_map/ppermute | solution.py:64
  137.7 37.7 %collective-permute-start.30 = (bf16[280,768]{1,0:T(8,128)(2,1)S(1)}, bf16[280,768]{1,0:T(8,128)(2,1)}, u32[]{:S(2)}, u32[]{:S(2)}) collective-permute-start(bf16[280,768]{1,0:T(8,128)(2,1)S(1)} %slice.94), channel_id=1, source_target_pairs={{0,8},{8,0},{16,24},{24,16},{1,9},{9,1},{17,25},{25,17},{2,10},{10... | collective-permute-start | bytes 1290248 | tf_op jit(solution)/shard_map/ppermute | solution.py:64
  153.5 22.0 %collective-permute-start.33 = (bf16[280,768]{1,0:T(8,128)(2,1)S(1)}, bf16[280,768]{1,0:T(8,128)(2,1)}, u32[]{:S(2)}, u32[]{:S(2)}) collective-permute-start(bf16[280,768]{1,0:T(8,128)(2,1)S(1)} %slice.95), channel_id=1, source_target_pairs={{0,16},{8,24},{16,0},{24,8},{1,17},{9,25},{17,1},{25,9},{2,18},{10... | collective-permute-start | bytes 1290248 | tf_op jit(solution)/shard_map/ppermute | solution.py:64
  155.6 19.9 %collective-permute-start.34 = (bf16[280,768]{1,0:T(8,128)(2,1)S(1)}, bf16[280,768]{1,0:T(8,128)(2,1)}, u32[]{:S(2)}, u32[]{:S(2)}) collective-permute-start(bf16[280,768]{1,0:T(8,128)(2,1)S(1)} %slice.96), channel_id=1, source_target_pairs={{0,8},{8,0},{16,24},{24,16},{1,9},{9,1},{17,25},{25,17},{2,10},{10... | collective-permute-start | bytes 1290248 | tf_op jit(solution)/shard_map/ppermute | solution.py:64
  157.4 16.2 %all-to-all-start.1 = ((bf16[128,4,384]{2,0,1:T(8,128)(2,1)}), bf16[128,4,384]{2,0,1:T(8,128)(2,1)S(1)}, u32[]{:S(2)}, u32[]{:S(2)}) async-start(bf16[128,4,384]{2,0,1:T(8,128)(2,1)} %bitcast.46), calls=%async_computation.1 | async-start | bytes 786432 | tf_op jit(solution)/shard_map/all_to_all | solution.py:732
  160.8 83.6 %reduce-scatter.6.cloned.1.call-start = ((), (), s32[]{:S(2)}) async-start(), calls=%async_computation.9 | async-start | bytes 3538944 | tf_op jit(solution)/shard_map/reduce_scatter | solution.py:844
  199.7 121.9 %reduce-scatter.4.cloned.1.call-start = ((), (), s32[]{:S(2)}) async-start(), calls=%async_computation.8 | async-start | bytes 3538944 | tf_op jit(solution)/shard_map/reduce_scatter | solution.py:857
  215.4 130.7 %reduce-scatter.8.cloned.1.call-start = ((), (), s32[]{:S(2)}) async-start(), calls=%async_computation.10 | async-start | bytes 3096576 | tf_op jit(solution)/shard_map/reduce_scatter | solution.py:910
  216.4 16.8 %collective-permute-start.35 = (bf16[1,280,768]{2,1,0:T(8,128)(2,1)S(1)}, bf16[1,280,768]{2,1,0:T(8,128)(2,1)S(1)}, u32[]{:S(2)}, u32[]{:S(2)}) collective-permute-start(bf16[1,280,768]{2,1,0:T(8,128)(2,1)S(1)} %copy-done.58), channel_id=1, source_target_pairs={{0,16},{8,24},{16,0},{24,8},{1,17},{9,25},{17,1},{25,9},{2,18},{10... | collective-permute-start | bytes 1290248 | tf_op jit(solution)/shard_map/ppermute | solution.py:64
  230.5 12.8 %collective-permute-start.36 = (bf16[1,280,768]{2,1,0:T(8,128)(2,1)S(1)}, bf16[1,280,768]{2,1,0:T(8,128)(2,1)S(1)}, u32[]{:S(2)}, u32[]{:S(2)}) collective-permute-start(bf16[1,280,768]{2,1,0:T(8,128)(2,1)S(1)} %copy-done.57), channel_id=1, source_target_pairs={{0,8},{8,0},{16,24},{24,16},{1,9},{9,1},{17,25},{25,17},{2,10},{10... | collective-permute-start | bytes 1290248 | tf_op jit(solution)/shard_map/ppermute | solution.py:64
  232.1 29.8 %collective-permute-start.37 = (bf16[2,280,768]{2,1,0:T(8,128)(2,1)}, bf16[2,280,768]{2,1,0:T(8,128)(2,1)S(1)}, u32[]{:S(2)}, u32[]{:S(2)}) collective-permute-start(bf16[2,280,768]{2,1,0:T(8,128)(2,1)} %get-tuple-element.110), channel_id=1, source_target_pairs={{0,16},{8,24},{16,0},{24,8},{1,17},{9,25},{17,1},{25,9},{2,18},{10... | collective-permute-start | bytes 2580488 | tf_op jit(solution)/shard_map/ppermute | solution.py:64
  232.6 30.7 %collective-permute-start.38 = (bf16[2,280,768]{2,1,0:T(8,128)(2,1)}, bf16[2,280,768]{2,1,0:T(8,128)(2,1)S(1)}, u32[]{:S(2)}, u32[]{:S(2)}) collective-permute-start(bf16[2,280,768]{2,1,0:T(8,128)(2,1)} %get-tuple-element.112), channel_id=1, source_target_pairs={{0,8},{8,0},{16,24},{24,16},{1,9},{9,1},{17,25},{25,17},{2,10},{10... | collective-permute-start | bytes 2580488 | tf_op jit(solution)/shard_map/ppermute | solution.py:64
  259.7 27.2 %collective-permute-start.43 = (bf16[128,3072]{1,0:T(8,128)(2,1)}, bf16[128,3072]{1,0:T(8,128)(2,1)S(1)}, u32[]{:S(2)}, u32[]{:S(2)}) collective-permute-start(bf16[128,3072]{1,0:T(8,128)(2,1)} %get-tuple-element.121.refs_0_.refs_2_), channel_id=1, source_target_pairs={{0,8},{8,0},{16,24},{24,16},{1,9},{9,1},{17,25},{25,17},{2,10},{10... | collective-permute-start | bytes 2359304 | tf_op jit(solution)/shard_map/ppermute | solution.py:64
  261.3 26.1 %collective-permute-start.44 = (bf16[128,3072]{1,0:T(8,128)(2,1)}, bf16[128,3072]{1,0:T(8,128)(2,1)S(1)}, u32[]{:S(2)}, u32[]{:S(2)}) collective-permute-start(bf16[128,3072]{1,0:T(8,128)(2,1)} %get-tuple-element.121.refs_0_.refs_2_), channel_id=1, source_target_pairs={{0,16},{8,24},{16,0},{24,8},{1,17},{9,25},{17,1},{25,9},{2,18},{10... | collective-permute-start | bytes 2359304 | tf_op jit(solution)/shard_map/ppermute | solution.py:64
  268.3 13.7 %collective-permute-start.40 = (bf16[128,512]{1,0:T(8,128)(2,1)}, bf16[128,512]{1,0:T(8,128)(2,1)S(1)}, u32[]{:S(2)}, u32[]{:S(2)}) collective-permute-start(bf16[128,512]{1,0:T(8,128)(2,1)} %get-tuple-element.116), channel_id=1, source_target_pairs={{0,8},{8,0},{16,24},{24,16},{1,9},{9,1},{17,25},{25,17},{2,10},{10... | collective-permute-start | bytes 393224 | tf_op jit(solution)/shard_map/ppermute | solution.py:64
  268.8 15.5 %collective-permute-start.41 = (bf16[128,512]{1,0:T(8,128)(2,1)}, bf16[128,512]{1,0:T(8,128)(2,1)S(1)}, u32[]{:S(2)}, u32[]{:S(2)}) collective-permute-start(bf16[128,512]{1,0:T(8,128)(2,1)} %get-tuple-element.117), channel_id=1, source_target_pairs={{0,16},{8,24},{16,0},{24,8},{1,17},{9,25},{17,1},{25,9},{2,18},{10... | collective-permute-start | bytes 393224 | tf_op jit(solution)/shard_map/ppermute | solution.py:64
  270.2 14.1 %collective-permute-start.42 = (bf16[128,512]{1,0:T(8,128)(2,1)}, bf16[128,512]{1,0:T(8,128)(2,1)S(1)}, u32[]{:S(2)}, u32[]{:S(2)}) collective-permute-start(bf16[128,512]{1,0:T(8,128)(2,1)} %get-tuple-element.118), channel_id=1, source_target_pairs={{0,24},{8,16},{16,8},{24,0},{1,25},{9,17},{17,9},{25,1},{2,26},{10... | collective-permute-start | bytes 393224 | tf_op jit(solution)/shard_map/ppermute | solution.py:64
  286.9 14.0 %collective-permute-start.45 = (bf16[128,1536]{1,0:T(8,128)(2,1)S(1)}, bf16[128,1536]{1,0:T(8,128)(2,1)S(1)}, u32[]{:S(2)}, u32[]{:S(2)}) collective-permute-start(bf16[128,1536]{1,0:T(8,128)(2,1)S(1)} %slice.81), channel_id=1, source_target_pairs={{0,16},{8,24},{16,0},{24,8},{1,17},{9,25},{17,1},{25,9},{2,18},{10... | collective-permute-start | bytes 1179656 | tf_op jit(solution)/shard_map/ppermute | solution.py:64
  287.5 13.4 %collective-permute-start.46 = (bf16[128,1536]{1,0:T(8,128)(2,1)S(1)}, bf16[128,1536]{1,0:T(8,128)(2,1)S(1)}, u32[]{:S(2)}, u32[]{:S(2)}) collective-permute-start(bf16[128,1536]{1,0:T(8,128)(2,1)S(1)} %slice.82), channel_id=1, source_target_pairs={{0,8},{8,0},{16,24},{24,16},{1,9},{9,1},{17,25},{25,17},{2,10},{10... | collective-permute-start | bytes 1179656 | tf_op jit(solution)/shard_map/ppermute | solution.py:64
  289.1 10.6 %collective-permute-start.47 = (bf16[128,512]{1,0:T(8,128)(2,1)}, bf16[128,512]{1,0:T(8,128)(2,1)S(1)}, u32[]{:S(2)}, u32[]{:S(2)}) collective-permute-start(bf16[128,512]{1,0:T(8,128)(2,1)} %get-tuple-element.119.refs_1_.refs_7_), channel_id=1, source_target_pairs={{0,8},{8,0},{16,24},{24,16},{1,9},{9,1},{17,25},{25,17},{2,10},{10... | collective-permute-start | bytes 393224 | tf_op jit(solution)/shard_map/ppermute | solution.py:64
  289.6 10.0 %collective-permute-start.48 = (bf16[128,512]{1,0:T(8,128)(2,1)}, bf16[128,512]{1,0:T(8,128)(2,1)S(1)}, u32[]{:S(2)}, u32[]{:S(2)}) collective-permute-start(bf16[128,512]{1,0:T(8,128)(2,1)} %get-tuple-element.119.refs_1_.refs_7_), channel_id=1, source_target_pairs={{0,16},{8,24},{16,0},{24,8},{1,17},{9,25},{17,1},{25,9},{2,18},{10... | collective-permute-start | bytes 393224 | tf_op jit(solution)/shard_map/ppermute | solution.py:64
  291.2 9.7 %collective-permute-start.49 = (bf16[128,512]{1,0:T(8,128)(2,1)}, bf16[128,512]{1,0:T(8,128)(2,1)S(1)}, u32[]{:S(2)}, u32[]{:S(2)}) collective-permute-start(bf16[128,512]{1,0:T(8,128)(2,1)} %get-tuple-element.119.refs_1_.refs_7_), channel_id=1, source_target_pairs={{0,24},{8,16},{16,8},{24,0},{1,25},{9,17},{17,9},{25,1},{2,26},{10... | collective-permute-start | bytes 393224 | tf_op jit(solution)/shard_map/ppermute | solution.py:64
  316.8 40.8 %collective-permute-start.55 = (bf16[2,280,1536]{2,1,0:T(8,128)(2,1)}, bf16[2,280,1536]{2,1,0:T(8,128)(2,1)S(1)}, u32[]{:S(2)}, u32[]{:S(2)}) collective-permute-start(bf16[2,280,1536]{2,1,0:T(8,128)(2,1)} %add_convert_fusion.1), channel_id=1, source_target_pairs={{0,8},{8,0},{16,24},{24,16},{1,9},{9,1},{17,25},{25,17},{2,10},{10... | collective-permute-start | bytes 5160968 | tf_op jit(solution)/shard_map/ppermute | solution.py:64
  318.4 40.8 %collective-permute-start.56 = (bf16[2,280,1536]{2,1,0:T(8,128)(2,1)}, bf16[2,280,1536]{2,1,0:T(8,128)(2,1)}, u32[]{:S(2)}, u32[]{:S(2)}) collective-permute-start(bf16[2,280,1536]{2,1,0:T(8,128)(2,1)} %add_convert_fusion), channel_id=1, source_target_pairs={{0,16},{8,24},{16,0},{24,8},{1,17},{9,25},{17,1},{25,9},{2,18},{10... | collective-permute-start | bytes 5160968 | tf_op jit(solution)/shard_map/ppermute | solution.py:64
  321.6 48.8 %collective-permute-start.57 = (bf16[1,280,1536]{2,1,0:T(8,128)(2,1)}, bf16[1,280,1536]{2,1,0:T(8,128)(2,1)}, u32[]{:S(2)}, u32[]{:S(2)}) collective-permute-start(bf16[1,280,1536]{2,1,0:T(8,128)(2,1)} %add_convert_fusion.3), channel_id=1, source_target_pairs={{0,8},{8,0},{16,24},{24,16},{1,9},{9,1},{17,25},{25,17},{2,10},{10... | collective-permute-start | bytes 2580488 | tf_op jit(solution)/shard_map/ppermute | solution.py:64
  322.1 48.2 %collective-permute-start.58 = (bf16[1,280,1536]{2,1,0:T(8,128)(2,1)}, bf16[1,280,1536]{2,1,0:T(8,128)(2,1)}, u32[]{:S(2)}, u32[]{:S(2)}) collective-permute-start(bf16[1,280,1536]{2,1,0:T(8,128)(2,1)} %add_convert_fusion.2), channel_id=1, source_target_pairs={{0,16},{8,24},{16,0},{24,8},{1,17},{9,25},{17,1},{25,9},{2,18},{10... | collective-permute-start | bytes 2580488 | tf_op jit(solution)/shard_map/ppermute | solution.py:64
  325.2 10.8 %collective-permute-start.54 = (f32[1,3584]{1,0:T(1,128)S(1)}, f32[1,3584]{1,0:T(1,128)S(1)}, u32[]{:S(2)}, u32[]{:S(2)}) collective-permute-start(f32[1,3584]{1,0:T(1,128)S(1)} %add.134), channel_id=1, source_target_pairs={{0,2},{1,3},{2,0},{3,1},{4,6},{5,7},{6,4},{7,5},{8,10},{9,11},{10,... | collective-permute-start | bytes 43016 | tf_op jit(solution)/shard_map/ppermute | solution.py:699
  (79 other events, 639.3 us)
Sparse Core Ops, SparseCore 0:
  10.5 28.9 all-gather.5
  45.1 52.4 all-gather.11
  99.2 37.4 all-gather.9
  138.3 37.1 all-gather.7
  199.8 39.2 reduce-scatter.5
  241.3 39.4 reduce-scatter.3
  309.0 37.1 reduce-scatter.7
